TPU v7x, 32 devices: a whole 2x2x4 slice. The times are simulated.
32 devices in a mesh: frame: 8 (over z, y), coil: 4 (over x, core).
Axes of the slice: x: 2, y: 2, z: 4, core: 2. Of those that a mesh axis runs over, the one named last changes fastest.
Arguments:
- spatial: float32 [8, 2, 320, 320], P(None, None, 'coil', 'frame'), may hold values from -6 to 6
- temporal: float32 [16, 8], P('frame'), may hold values from -2 to 2
- sensitivity: bfloat16 [8, 2, 320, 320], P('coil'), may hold values from -5 to 5
- coil_data: bfloat16 [16, 8, 2, 320, 320], P('frame', 'coil'), may hold values from -6 to 6
- kernel_index: int32 [16, 640, 640], P('frame'), may hold values from 0 to 7
- kernel_level: float32 [16, 8], P('frame'), may hold values from 0.02 to 4
Outputs:
- spatial_next: float32 [8, 2, 320, 320], P(None, None, 'coil', 'frame')
- images: bfloat16 [16, 2, 320, 320], P('frame')
All inputs are finite; a program needn't handle non-finite values.
Results may differ from a plain program's by a relative error of at most 0.001.
Values may be sent and summed in bfloat16 or wider, within the bound.
No kernel may reach another device: no remote copies, remote signals or barrier semaphores. Data moves between devices by JAX's collectives and lax.ppermute only.
A program may use at most 128 MiB of HBM per device.

v0:
```python
import functools
import jax, jax.numpy as jnp, numpy as np
from jax import lax
from jax.sharding import PartitionSpec as P
from jax.experimental import pallas as pl
from jax.experimental.pallas import tpu as pltpu

LANES = 128
VMEM_BYTES = 67043328
F32, BF16 = jnp.float32, jnp.bfloat16


def halves(table):
    high = np.asarray(table, np.float32).astype(BF16)
    low = (table - high.astype(np.float64)).astype(np.float32).astype(BF16)
    return high, low


def wave(count, places, period):
    turns = np.outer(np.arange(count), places) % (2 * period)
    slot = np.outer([period // 2], places) % (2 * period)
    angle = np.pi / period * turns
    cosine, sine = np.cos(angle), np.sin(angle)
    sine[0] = np.sin(np.pi / period * slot[0])
    return cosine, sine


def row_tables(rows, period):
    cosine, sine = wave(rows, 2 * np.arange(rows // 2) + 1, period)
    forward, inverse = [], []
    for table in (cosine, sine):
        high, low = halves(table)
        forward.append(np.concatenate([high, high, low], 1))
        inverse.append(np.concatenate([high.T, high.T, low.T], 1))
    return np.stack(forward), np.stack(inverse)


def col_tables(cols, period):
    main = cols // LANES * LANES
    cosine, sine = wave(cols, 2 * np.arange(cols) - (cols - 1), period)
    mixed = np.concatenate([cosine[:main], sine[:main], cosine[main:], sine[main:]], 0).T
    high, low = halves(mixed)
    blank = np.zeros((cols - main, mixed.shape[1]), BF16)
    forward = np.concatenate([high[:main], high[:main], low[:main], high[main:], high[main:], low[main:], blank], 0)
    high, low = high.T, low.T
    inverse = np.concatenate([high, high, low], 0)
    return forward, inverse


def split(value):
    high = value.astype(BF16)
    return high, (value - high.astype(F32)).astype(BF16)


def dot(left, right):
    return jnp.dot(left, right, preferred_element_type=F32)


def normal_kernel(size, extra, frame, first_coil, me_ref, *refs):
    parts, refs = refs[:size], refs[size:]
    sens_hbm, sig_hbm, dif_hbm, data_hbm, tcol_hbm, trow_hbm, tback_hbm, tlast_hbm, sig0_ref, rev_ref = refs[:10]
    before, refs = refs[10 : 10 + extra], refs[10 + extra :]
    blocks, refs = refs[:size], refs[size:]
    sens_ref, tcol_ref, trow_ref, sig_ref, dif_ref, tback_ref, tlast_ref, data_ref, sems = refs[:9]
    img_n, img_s, xcat, mid, back, last, acc = refs[9:]
    chosen = pl.ds(first_coil, sens_ref.shape[0])
    moved = [
        pltpu.make_async_copy(source, target, sems.at[n])
        for n, (source, target) in enumerate((
            (sens_hbm.at[chosen], sens_ref), (tcol_hbm, tcol_ref), (trow_hbm, trow_ref), (sig_hbm.at[frame], sig_ref), (dif_hbm.at[frame], dif_ref),
            (tback_hbm, tback_ref), (tlast_hbm, tlast_ref), (data_hbm.at[frame, chosen], data_ref),
        ))
    ]
    for copy in moved:
        copy.start()
    coils, _, rows, _ = sens_ref.shape
    cols = acc.shape[2]
    half = rows // 2
    main = cols // LANES * LANES
    spectral = tcol_ref.shape[1]
    steps = spectral // LANES
    count = rows // size

    def place(number):
        return pl.ds(pl.multiple_of((me_ref[0] ^ number) * count, count), count)

    for number in range(size):
        for part in range(2):
            img_n[part, place(number)] = parts[number][part]
    for part in range(2):
        for top, value in enumerate((img_n[part, half:].astype(F32), dot(rev_ref[...], img_n[part, :half]))):
            here = slice(top * half, top * half + half)
            img_s[part, here, :main] = value[:, :main]
            img_s[part, here, main:] = jnp.concatenate([value[:, main:]] * (LANES // (cols - main)), 1)
    moved[0].wait()
    lane = lax.broadcasted_iota(jnp.int32, (half, LANES), 1)
    keep = (lane > 0).astype(F32)
    low_lane = lane < (cols - main)

    def one_coil(coil, carry):
        sums = {}
        for top in range(2):
            here = slice(top * half, top * half + half)
            s_re = sens_ref[coil, 0, here].astype(F32)
            s_im = sens_ref[coil, 1, here].astype(F32)
            i_re, i_im = img_s[0, here], img_s[1, here]
            sums[top, 0] = s_re * i_re - s_im * i_im
            sums[top, 1] = s_re * i_im + s_im * i_re
        for part in range(2):
            for sign in range(2):
                value = sums[0, part] + sums[1, part] if sign == 0 else sums[0, part] - sums[1, part]
                high, low = split(value)
                there = slice((2 * sign + part) * half, (2 * sign + part + 1) * half)
                xcat[there, :main] = high[:, :main]
                xcat[there, main : 2 * main] = low[:, :main]
                xcat[there, 2 * main : 2 * main + LANES] = jnp.where(low_lane, high[:, main:], low[:, main:])
                xcat[there, 2 * main + LANES :] = high[:, main:]

        @pl.when(coil == 0)
        def _():
            moved[1].wait()

        for sign in range(2):
            lines = slice(2 * sign * half, (2 * sign + 2) * half)
            spread = [xcat[lines, : 2 * main], xcat[lines, :main], xcat[lines, 2 * main :]]
            both = dot(jnp.concatenate(spread, 1), tcol_ref[...])
            re, im = both[:half], both[half:]
            for step in range(steps):
                at = step * LANES
                if at < main:
                    c_re, c_im = re[:, at : at + LANES], im[:, at : at + LANES]
                    s_re, s_im = re[:, main + at : main + at + LANES], im[:, main + at : main + at + LANES]
                    if at == 0:
                        s_re, s_im = s_re * keep, s_im * keep
                    m_re, m_im = c_re + s_im, c_im - s_re
                elif at < 2 * main:
                    c_re, c_im = re[:, at - main : at - main + LANES], im[:, at - main : at - main + LANES]
                    s_re, s_im = re[:, at : at + LANES], im[:, at : at + LANES]
                    if at == main:
                        c_re, c_im = c_re * keep, c_im * keep
                    m_re, m_im = c_re - s_im, c_im + s_re
                else:
                    g_re, g_im = re[:, at : at + LANES], im[:, at : at + LANES]
                    m_re = g_re + pltpu.roll(g_im, LANES // 2, 1)
                    m_im = g_im - pltpu.roll(g_re, LANES // 2, 1)
                for part, value in enumerate((m_re, m_im)):
                    high, low = split(value)
                    there = slice((2 * step + part) * LANES, (2 * step + part + 1) * LANES)
                    mid[sign, :half, there] = high
                    mid[sign, half:, there] = low

        @pl.when(coil == 0)
        def _():
            for copy in moved[2:6]:
                copy.wait()

        def one_step(step, carry):
            there = pl.ds(pl.multiple_of(step * 2 * LANES, 2 * LANES), 2 * LANES)
            here = pl.ds(pl.multiple_of(step * LANES, LANES), LANES)
            even, odd = [
                dot(trow_ref[sign], jnp.concatenate([mid[sign, :, there], mid[sign, :half, there]], 0)) for sign in range(2)
            ]
            sig, dif = sig_ref[:, here], dif_ref[:, here]
            c_re, c_im = even[:, :LANES], even[:, LANES:]
            s_re, s_im = odd[:, :LANES], odd[:, LANES:]
            p_re = sig * c_re + dif * s_im
            p_im = sig * c_im - dif * s_re
            q_re = sig * s_re - dif * c_im
            q_im = sig * s_im + dif * c_re
            first = sig0_ref[frame, :, here]
            q_re = jnp.concatenate([first * s_re[:8] - dif[:8] * c_im[:8], q_re[8:]], 0)
            q_im = jnp.concatenate([first * s_im[:8] + dif[:8] * c_re[:8], q_im[8:]], 0)
            for number, pair in enumerate(((p_re, p_im), (q_re, q_im))):
                both = [split(value) for value in pair]
                high, low = [jnp.concatenate([both[0][n], both[1][n]], 1) for n in range(2)]
                back[number, :, there] = dot(tback_ref[number], jnp.concatenate([high, low, high], 0))
            return carry

        lax.fori_loop(0, steps, one_step, 0, unroll=True)
        for sign in range(2):
            for step in range(steps):
                at = step * LANES

                def piece(index, part):
                    return back[sign, :, (2 * index + part) * LANES : (2 * index + part + 1) * LANES]

                shift = main // LANES
                if at < main:
                    u_re, u_im = piece(step, 0), piece(step, 1)
                    v_re, v_im = piece(step + shift, 0), piece(step + shift, 1)
                    if at == 0:
                        v_re, v_im = v_re * keep, v_im * keep
                    w_re, w_im = u_re + v_re, u_im + v_im
                elif at < 2 * main:
                    u_re, u_im = piece(step - shift, 0), piece(step - shift, 1)
                    v_re, v_im = piece(step, 0), piece(step, 1)
                    if at == main:
                        u_re, u_im = u_re * keep, u_im * keep
                    w_re, w_im = v_im - u_im, u_re - v_re
                else:
                    g_re, g_im = piece(step, 0), piece(step, 1)
                    w_re = g_re - pltpu.roll(g_im, LANES // 2, 1)
                    w_im = g_im + pltpu.roll(g_re, LANES // 2, 1)
                for part, value in enumerate((w_re, w_im)):
                    high, low = split(value)
                    there = slice((2 * sign + part) * half, (2 * sign + part + 1) * half)
                    last[there, at : at + LANES] = high
                    last[there, spectral + at : spectral + at + LANES] = low

        @pl.when(coil == 0)
        def _():
            moved[6].wait()
            moved[7].wait()

        final = dot(jnp.concatenate([last[...], last[:, :spectral]], 1), tlast_ref[...])
        plus_re, plus_im, minus_re, minus_im = [final[n * half : (n + 1) * half] for n in range(4)]
        for top in range(2):
            here = slice(top * half, top * half + half)
            n_re = plus_re + minus_re if top == 0 else plus_re - minus_re
            n_im = plus_im + minus_im if top == 0 else plus_im - minus_im
            if top == 0:
                d_re, d_im = data_ref[coil, 0, half:].astype(F32), data_ref[coil, 1, half:].astype(F32)
            else:
                d_re, d_im = dot(rev_ref[...], data_ref[coil, 0, :half]), dot(rev_ref[...], data_ref[coil, 1, :half])
            n_re, n_im = n_re - d_re, n_im - d_im
            s_re = sens_ref[coil, 0, here, :cols].astype(F32)
            s_im = sens_ref[coil, 1, here, :cols].astype(F32)
            acc[0, here] += s_re * n_re + s_im * n_im
            acc[1, here] += s_re * n_im - s_im * n_re
        return carry

    acc[...] = jnp.zeros_like(acc)
    lax.fori_loop(0, coils, one_coil, 0)
    for part in range(2):
        above, below = acc[part, :half], acc[part, half:]
        high, low = split(below)
        rest = (below - high.astype(F32) - low.astype(F32)).astype(BF16)
        turned = dot(rev_ref[...], high) + dot(rev_ref[...], low) + dot(rev_ref[...], rest)
        acc[part, half:] = above
        acc[part, :half] = turned
    for number in range(size):
        for part in range(2):
            value = acc[part, place(number)]
            blocks[number][part] = value + before[number][part] if extra == size else value


def normal_call(frame, chosen, me, parts, sens, sig, dif, sig0, data, tables, before):
    size = len(parts)
    rows, wide = sens.shape[2:]
    coils = len(chosen)
    cols = data.shape[4]
    half = rows // 2
    tcol, tlast, trow, tback, rev = tables
    spectral = tcol.shape[1]
    held = pl.BlockSpec(memory_space=pltpu.VMEM)
    away = pl.BlockSpec(memory_space=pl.ANY)
    like = lambda value: pltpu.VMEM(value.shape, value.dtype)
    one = lambda value: pltpu.VMEM(value.shape[1:], value.dtype)
    some = lambda value: pltpu.VMEM((coils,) + value.shape[1:], value.dtype)
    flops = 2 * coils * 2 * 12 * rows * cols * spectral

    return pl.pallas_call(
        functools.partial(normal_kernel, size, len(before), frame, chosen[0]),
        out_shape=[jax.ShapeDtypeStruct((2, rows // size, cols), F32)] * size,
        in_specs=[pl.BlockSpec(memory_space=pltpu.SMEM)] + [held] * size + [away] * 8 + [held] * 2 + [held if len(before) == size else away] * len(before),
        out_specs=[held] * size,
        scratch_shapes=[
            some(sens), like(tcol), like(trow), one(sig), one(dif), like(tback), like(tlast), some(one(data)),
            pltpu.SemaphoreType.DMA((8,)),
            pltpu.VMEM((2, rows, cols), BF16),
            pltpu.VMEM((2, rows, wide), F32),
            pltpu.VMEM((4 * half, tcol.shape[0] * 3 // 4), BF16),
            pltpu.VMEM((2, 2 * half, 2 * spectral), BF16),
            pltpu.VMEM((2, half, 2 * spectral), F32),
            pltpu.VMEM((4 * half, 2 * spectral), BF16),
            pltpu.VMEM((2, rows, cols), F32),
        ],
        compiler_params=pltpu.CompilerParams(vmem_limit_bytes=VMEM_BYTES),
        cost_estimate=pl.CostEstimate(flops=flops, bytes_accessed=8 * 1024 * 1024, transcendentals=0),
    )(me, *parts, sens, sig, dif, data, tcol, trow, tback, tlast, sig0, rev, *before)


def place_kernel(me_ref, *refs):
    size = len(refs) - 1
    parts, out_ref = refs[:size], refs[size]
    count = parts[0].shape[2]
    for number in range(size):
        for frame in range(out_ref.shape[0]):
            for part in range(2):
                there = pl.ds(pl.multiple_of((me_ref[0] ^ number) * count, count), count)
                out_ref[frame, part, there] = parts[number][frame, part]


def place_call(me, parts):
    frames, _, count, cols = parts[0].shape
    held = pl.BlockSpec(memory_space=pltpu.VMEM)
    return pl.pallas_call(
        place_kernel,
        out_shape=jax.ShapeDtypeStruct((frames, 2, count * len(parts), cols), parts[0].dtype),
        in_specs=[pl.BlockSpec(memory_space=pltpu.SMEM)] + [held] * len(parts),
        out_specs=held,
    )(me, *parts)


def freq_order_rows(rows, period):
    k = np.arange(rows)
    return np.concatenate([k, np.where(k == 0, period // 2, period - k)])


def freq_order_cols(cols, period):
    main = cols // LANES * LANES
    l = np.arange(cols)
    u, v = l, np.where(l == 0, period // 2, period - l)
    return np.concatenate([u[:main], v[:main], u[main:], v[main:]])


def prepare_kernel(index_ref, level_ref, sens_ref, row_ref, col_ref, rev_ref, dup_ref, after_ref, sig_ref, dif_ref, sig0_ref, out_ref):
    frame = pl.program_id(0)
    rows = sig_ref.shape[1]
    half = rows // 2
    levels = level_ref.shape[1]
    scale = 1.0 / (index_ref.shape[1] * index_ref.shape[2])

    def values(index):
        place = dot(index, col_ref[...])
        kernel = jnp.full(place.shape, level_ref[frame, 0] * scale, F32)
        for number in range(1, levels):
            kernel = jnp.where(place > number - 0.5, level_ref[frame, number] * scale, kernel)
        return kernel

    upper = values(index_ref[0, :rows].astype(F32).astype(BF16))
    turned = dot(row_ref[...], index_ref[0, rows:].astype(F32).astype(BF16))
    lower = values(turned.astype(BF16))
    first = lax.broadcasted_iota(jnp.int32, upper[:8].shape, 0) == 0
    sig_ref[0] = upper + lower
    dif_ref[0] = upper - lower
    sig_ref[0, :8] = jnp.where(first, upper[:8], upper[:8] + lower[:8])
    sig0_ref[0] = jnp.where(first, lower[:8], upper[:8] + lower[:8])
    dif_ref[0, :8] = jnp.where(first, 0.0, upper[:8] - lower[:8])

    for part in range(2):
        wide = dot(sens_ref[0, part], dup_ref[...]).astype(BF16)
        out_ref[0, part, :half] = wide[half:]
        out_ref[0, part, half:] = dot(rev_ref[...], wide[:half]).astype(BF16)


def prepare_call(index, level, sens, perms, after):
    frames, rows_pad, cols_pad = index.shape
    coils, _, rows, cols = sens.shape
    row, col, rev, dup = perms
    whole = lambda n: (lambda f: (0,) * n)
    block = lambda *shape: pl.BlockSpec((1,) + shape, lambda f: (f,) + (0,) * len(shape))
    return pl.pallas_call(
        prepare_kernel,
        grid=(frames,),
        out_shape=(
            jax.ShapeDtypeStruct((frames, rows, cols_pad), F32),
            jax.ShapeDtypeStruct((frames, rows, cols_pad), F32),
            jax.ShapeDtypeStruct((frames, 8, cols_pad), F32),
            jax.ShapeDtypeStruct((coils, 2, rows, dup.shape[1]), BF16),
        ),
        in_specs=[
            block(rows_pad, cols_pad),
            pl.BlockSpec(memory_space=pltpu.SMEM),
            block(2, rows, cols),
            pl.BlockSpec(row.shape, whole(2)),
            pl.BlockSpec(col.shape, whole(2)),
            pl.BlockSpec(rev.shape, whole(2)),
            pl.BlockSpec(dup.shape, whole(2)),
            pl.BlockSpec(memory_space=pl.ANY),
        ],
        out_specs=(block(rows, cols_pad), block(rows, cols_pad), block(8, cols_pad), block(2, rows, dup.shape[1])),
        compiler_params=pltpu.CompilerParams(vmem_limit_bytes=VMEM_BYTES),
        cost_estimate=pl.CostEstimate(flops=6 * frames * rows * cols_pad * cols_pad, bytes_accessed=16 * 1024 * 1024, transcendentals=0),
    )(index, level, sens, row, col, rev, dup, after)


STEP_SIZE = 0.15


def one_hot(order):
    return (order[:, None] == np.arange(len(order))[None, :]).astype(BF16)


def constants(rows, cols, rows_pad, cols_pad):
    assert rows_pad == 2 * rows and cols_pad == 2 * cols
    main = cols // LANES * LANES
    assert 2 * (cols - main) == LANES and rows % 32 == 0
    forward, inverse = row_tables(rows, rows_pad)
    first, last = col_tables(cols, cols_pad)
    turn = np.arange(rows // 2)[::-1]
    flip = freq_order_rows(rows, rows_pad)[rows:] - rows
    spread = np.concatenate([np.arange(cols), np.arange(main, cols)])
    rev, row = one_hot(turn), one_hot(flip)
    col = one_hot(freq_order_cols(cols, cols_pad)).T
    dup = (np.arange(cols)[:, None] == spread[None, :]).astype(BF16)
    tables = [jnp.asarray(t) for t in (first, last, forward, inverse, rev)]
    return tables, [jnp.asarray(t) for t in (row, col, rev, dup)]


def exchange(value, axis, distance):
    size = lax.axis_size(axis)
    return lax.ppermute(value, axis, [(i, i ^ distance) for i in range(size)])


def gather_blocks(own, axis):
    held = {0: own}
    distance = lax.axis_size(axis) // 2
    while distance:
        for key in list(held):
            held[key ^ distance] = exchange(held[key], axis, distance)
        distance //= 2
    return [held[key] for key in sorted(held)]


def gather_direct(own, axis):
    return [own] + [exchange(own, axis, distance) for distance in range(1, lax.axis_size(axis))]


def scatter_blocks(blocks, axis):
    held = dict(enumerate(blocks))
    distance = 1
    while distance < lax.axis_size(axis):
        held = {
            key: value + exchange(held[key ^ distance], axis, distance)
            for key, value in held.items()
            if not key & distance
        }
        distance *= 2
    return held[0]


def scatter_direct(blocks, axis):
    total = blocks[0]
    for distance in range(1, lax.axis_size(axis)):
        total = total + exchange(blocks[distance], axis, distance)
    return total


def gather_small(value, axis):
    size = lax.axis_size(axis)
    me = lax.axis_index(axis)
    held = value[None]
    distance = 1
    while distance < size:
        other = exchange(held, axis, distance)
        upper = (me // distance) % 2 == 1
        held = jnp.where(upper, jnp.concatenate([other, held]), jnp.concatenate([held, other]))
        distance *= 2
    return held


def make_images(factors, temporal_all):
    mixed = jnp.einsum("ftr,rcxy->ftcxy", temporal_all, factors, precision=lax.Precision.HIGHEST)
    return mixed.astype(BF16)


def send_images(images):
    images = images.reshape((-1,) + images.shape[2:])
    return lax.all_to_all(images, "frame", split_axis=0, concat_axis=3, tiled=True)


def send_residual(value):
    return lax.all_to_all(value[None], "frame", split_axis=3, concat_axis=0, tiled=True)


def body(spatial, temporal, sensitivity, coil_data, kernel_index, kernel_level):
    rows, cols = sensitivity.shape[2:]
    tables, perms = constants(rows, cols, kernel_index.shape[1], kernel_index.shape[2])
    me = lax.axis_index("coil").astype(jnp.int32)[None]
    temporal_all = gather_small(temporal, "frame")
    images = make_images(spatial, temporal_all)
    own = send_images(images)
    frames = own.shape[0]

    sig, dif, sig0, wide = prepare_call(kernel_index, kernel_level, sensitivity, perms, images)
    blocks = []
    coils = list(range(sensitivity.shape[0]))
    for frame in range(frames):
        parts = (gather_direct if frame else gather_blocks)(own[frame], "coil")
        groups = [coils[:1], coils[1:]] if frame and len(coils) > 1 else [coils]
        before = blocks[-1][:1] if blocks else []
        for group in groups:
            before = normal_call(frame, group, me, parts, wide, sig, dif, sig0, coil_data, tables, before)
        blocks.append(before)
    gradient = 0.0
    for frame in range(frames):
        final = frame == frames - 1
        rows_sum = (scatter_blocks if final else scatter_direct)(blocks[frame], "coil")
        residual = send_residual(rows_sum)
        gradient = gradient + jnp.einsum(
            "fr,fcxy->rcxy", temporal_all[:, frame], residual, precision=lax.Precision.HIGHEST
        )
    spatial_next = spatial - STEP_SIZE * gradient
    parts = gather_blocks(send_images(make_images(spatial_next, temporal_all)), "coil")
    return spatial_next, place_call(me, parts)


def solution(mesh):
    placed = (
        P(None, None, "coil", "frame"),
        P("frame", None),
        P("coil", None, None, None),
        P("frame", "coil", None, None, None),
        P("frame", None, None),
        P("frame", None),
    )
    return jax.shard_map(
        body,
        mesh=mesh,
        in_specs=placed,
        out_specs=(P(None, None, "coil", "frame"), P("frame", None, None, None)),
        check_vma=False,
    )
```

profile of v0, /device:TPU:0, one launch (start us, length us, event | category | flops | bytes accessed | tf_op | source)
XLA Modules:
  0.0 159.1 jit_solution(14720096385279906994)
XLA Ops:
  0.6 3.1 %collective-permute-start = (f32[1,2,8]{2,1,0:T(2,128)}, f32[1,2,8]{2,1,0:T(2,128)S(1)}, u32[]{:S(2)}, u32[]{:S(2)}) collective-permute-start(f32[1,2,8]{2,1,0:T(2,128)} %bitcast.58), channel_id=1, source_target_pairs={{0,4},{4,0},{8,12},{12,8},{16,20},{20,16},{24,28},{28,24},{1,5},{5... | collective-permute-start | bytes 200 | tf_op jit(solution)/shard_map/ppermute | solution.py:403
  3.7 1.8 %collective-permute-done = f32[1,2,8]{2,1,0:T(2,128)S(1)} collective-permute-done((f32[1,2,8]{2,1,0:T(2,128)}, f32[1,2,8]{2,1,0:T(2,128)S(1)}, u32[]{:S(2)}, u32[]{:S(2)}) %collective-permute-start) | collective-permute-done | bytes 96 | tf_op jit(solution)/shard_map/ppermute | solution.py:403
  6.2 2.1 %collective-permute-start.1 = (f32[2,2,8]{2,1,0:T(2,128)S(1)}, f32[2,2,8]{2,1,0:T(2,128)S(1)}, u32[]{:S(2)}, u32[]{:S(2)}) collective-permute-start(f32[2,2,8]{2,1,0:T(2,128)S(1)} %maximum_select_fusion.2), channel_id=1, source_target_pairs={{0,8},{4,12},{8,0},{12,4},{16,24},{20,28},{24,16},{28,20},{1,9},{5... | collective-permute-start | bytes 392 | tf_op jit(solution)/shard_map/ppermute | solution.py:403
  8.3 1.6 collective-permute-done.1
  9.9 3.0 %collective-permute-start.2 = (f32[4,2,8]{2,1,0:T(2,128)S(1)}, f32[4,2,8]{2,1,0:T(2,128)S(1)}, u32[]{:S(2)}, u32[]{:S(2)}) collective-permute-start(f32[4,2,8]{2,1,0:T(2,128)S(1)} %maximum_select_fusion.1), channel_id=1, source_target_pairs={{0,16},{4,20},{8,24},{12,28},{16,0},{20,4},{24,8},{28,12},{1,17},{... | collective-permute-start | bytes 776 | tf_op jit(solution)/shard_map/ppermute | solution.py:403
  12.9 1.6 collective-permute-done.2
  15.1 1.6 %fusion.8 = bf16[8,2,2,80,40]{3,0,4,2,1:T(8,128)(2,1)S(1)} fusion(f32[8,2,80,40]{2,3,1,0:T(8,128)} %param.14, f32[8,2,8,1,1]{2,1,0,4,3:T(2,128)S(1)} %bitcast.54), kind=kOutput, calls=%fused_computation.10 | convolution fusion | flops 9830400 | bytes 410112 | tf_op jit(solution)/shard_map/ftr,rcxy->ftcxy/dot_general | solution.py:454
  18.2 15.0 %all_to_all.69 = bf16[16,2,80,40]{2,3,1,0:T(8,128)(2,1)S(1)} all-to-all(bf16[16,2,80,40]{2,3,1,0:T(8,128)(2,1)S(1)} %copy.57), channel_id=1, replica_groups=mesh['frame'=8,'coil'=4] {'frame'}, dimensions={0} | all-to-all | bytes 409600 | tf_op jit(solution)/shard_map/all_to_all | solution.py:460
  34.7 1.5 collective-permute-start.4
  36.2 3.7 %collective-permute-done.4.refs_2_ = bf16[2,80,320]{2,1,0:T(8,128)(2,1)} collective-permute-done((bf16[2,80,320]{2,1,0:T(8,128)(2,1)}, bf16[2,80,320]{2,1,0:T(8,128)(2,1)}, u32[]{:S(2)}, u32[]{:S(2)}) %collective-permute-start.4) | collective-permute-done | bytes 102432 | tf_op jit(solution)/shard_map/ppermute | solution.py:403
  39.9 7.1 %shard_map.149 = (f32[2,320,640]{2,1,0:T(8,128)}, f32[2,320,640]{2,1,0:T(8,128)}, f32[2,8,640]{2,1,0:T(8,128)}, bf16[2,2,320,384]{3,2,1,0:T(8,128)(2,1)}) custom-call(s32[2,640,640]{2,1,0:T(8,128)} %index_ref.1, f32[2,8]{1,0:T(2,128)} %level_ref.1, bf16[2,2,320,320]{3,2,1,0:T(8,128)(2,1)} %sens_ref.1, bf16[320,320]{1,0:T(8,128)(2,1)} %constant.83.clone.row_ref, ...), custom_call_target="tpu_custom_call" | custom-call | flops 1572864000 | bytes 16777216 | tf_op jit(solution)/shard_map/pallas_call | solution.py:353
  47.0 0.9 copy.66
  48.7 1.6 collective-permute-start.11
  50.8 16.3 %shard_map.150 = (f32[2,80,320]{2,1,0:T(8,128)}, f32[2,80,320]{2,1,0:T(8,128)}, f32[2,80,320]{2,1,0:T(8,128)}, f32[2,80,320]{2,1,0:T(8,128)}) custom-call(s32[1]{0:T(128)} %bitcast.3.me_ref, bf16[2,80,320]{2,1,0:T(8,128)(2,1)} %copy.61.refs_0_, bf16[2,80,320]{2,1,0:T(8,128)(2,1)} %collective-permute-done.3.refs_1_, ...), custom_call_target="tpu_custom_call" | custom-call | flops 6291456000 | bytes 8388608 | tf_op jit(solution)/shard_map/pallas_call | solution.py:262
  67.1 10.0 %shard_map.151 = (f32[2,80,320]{2,1,0:T(8,128)}, f32[2,80,320]{2,1,0:T(8,128)}, f32[2,80,320]{2,1,0:T(8,128)}, f32[2,80,320]{2,1,0:T(8,128)}) custom-call(s32[1]{0:T(128)} %bitcast.3.me_ref, bf16[2,80,320]{2,1,0:T(8,128)(2,1)} %copy.71.refs_0_, bf16[2,80,320]{2,1,0:T(8,128)(2,1)} %collective-permute-done.9.refs_1_, ...), custom_call_target="tpu_custom_call" | custom-call | flops 3145728000 | bytes 8388608 | tf_op jit(solution)/shard_map/pallas_call | solution.py:262
  77.1 10.3 %shard_map.152 = (f32[2,80,320]{2,1,0:T(8,128)}, f32[2,80,320]{2,1,0:T(8,128)}, f32[2,80,320]{2,1,0:T(8,128)}, f32[2,80,320]{2,1,0:T(8,128)}) custom-call(s32[1]{0:T(128)} %bitcast.3.me_ref, bf16[2,80,320]{2,1,0:T(8,128)(2,1)} %copy.71.refs_0_, bf16[2,80,320]{2,1,0:T(8,128)(2,1)} %collective-permute-done.9.refs_1_, ...), custom_call_target="tpu_custom_call" | custom-call | flops 3145728000 | bytes 8388608 | tf_op jit(solution)/shard_map/pallas_call | solution.py:262
  88.0 1.5 collective-permute-start.7
  90.2 1.0 add.41
  91.1 1.6 collective-permute-start.14
  92.7 4.4 %collective-permute-done.7 = f32[2,80,320]{2,1,0:T(8,128)S(1)} collective-permute-done((f32[2,80,320]{2,1,0:T(8,128)}, f32[2,80,320]{2,1,0:T(8,128)S(1)}, u32[]{:S(2)}, u32[]{:S(2)}) %collective-permute-start.7) | collective-permute-done | bytes 204832 | tf_op jit(solution)/shard_map/ppermute | solution.py:403
  97.1 4.4 %collective-permute-done.8 = f32[2,80,320]{2,1,0:T(8,128)S(1)} collective-permute-done((f32[2,80,320]{2,1,0:T(8,128)}, f32[2,80,320]{2,1,0:T(8,128)S(1)}, u32[]{:S(2)}, u32[]{:S(2)}) %collective-permute-start.8) | collective-permute-done | bytes 204832 | tf_op jit(solution)/shard_map/ppermute | solution.py:403
  101.4 1.0 add_bitcast_fusion.1
  102.5 0.9 copy.62
  103.3 3.8 %all-to-all-start.1 = ((f32[1,2,80,320]{2,1,0,3:T(2,128)}), f32[1,2,80,320]{2,1,0,3:T(2,128)S(1)}, u32[]{:S(2)}, u32[]{:S(2)}) async-start(f32[1,2,80,320]{2,1,0,3:T(2,128)} %copy.62), calls=%async_computation.1 | async-start | bytes 655360 | tf_op jit(solution)/shard_map/all_to_all | solution.py:464
  107.2 0.9 copy.72
  108.1 10.2 %all-to-all-done.1 = f32[1,2,80,320]{2,1,0,3:T(2,128)S(1)} async-done(((f32[1,2,80,320]{2,1,0,3:T(2,128)}), f32[1,2,80,320]{2,1,0,3:T(2,128)S(1)}, u32[]{:S(2)}, u32[]{:S(2)}) %all-to-all-start.1) | async-done | bytes 204832 | tf_op jit(solution)/shard_map/all_to_all | solution.py:464
  118.3 3.6 %all-to-all-start.2 = ((f32[1,2,80,320]{2,1,0,3:T(2,128)}), f32[1,2,80,320]{2,1,0,3:T(2,128)S(1)}, u32[]{:S(2)}, u32[]{:S(2)}) async-start(f32[1,2,80,320]{2,1,0,3:T(2,128)} %copy.72), calls=%async_computation.2 | async-start | bytes 655360 | tf_op jit(solution)/shard_map/all_to_all | solution.py:464
  122.4 10.0 %all-to-all-done.2 = f32[1,2,80,320]{2,1,0,3:T(2,128)S(1)} async-done(((f32[1,2,80,320]{2,1,0,3:T(2,128)}), f32[1,2,80,320]{2,1,0,3:T(2,128)S(1)}, u32[]{:S(2)}, u32[]{:S(2)}) %all-to-all-start.2) | async-done | bytes 204832 | tf_op jit(solution)/shard_map/all_to_all | solution.py:464
  133.7 14.3 %all_to_all.70 = bf16[16,2,80,40]{2,3,1,0:T(8,128)(2,1)S(1)} all-to-all(bf16[16,2,80,40]{2,3,1,0:T(8,128)(2,1)S(1)} %bitcast.49), channel_id=1, replica_groups=mesh['frame'=8,'coil'=4] {'frame'}, dimensions={0} | all-to-all | bytes 409600 | tf_op jit(solution)/shard_map/all_to_all | solution.py:460
  148.3 1.6 collective-permute-start.16
  149.9 4.7 %collective-permute-done.16.refs_2_ = bf16[2,2,80,320]{3,2,1,0:T(8,128)(2,1)S(1)} collective-permute-done((bf16[2,2,80,320]{3,2,1,0:T(8,128)(2,1)S(1)}, bf16[2,2,80,320]{3,2,1,0:T(8,128)(2,1)S(1)}, u32[]{:S(2)}, u32[]{:S(2)}) %collective-permute-start.16) | collective-permute-done | bytes 204832 | tf_op jit(solution)/shard_map/ppermute | solution.py:403
  156.8 2.3 %shard_map.153 = bf16[2,2,320,320]{3,2,1,0:T(8,128)(2,1)} custom-call(s32[1]{0:T(128)} %bitcast.3.me_ref, bf16[2,2,80,320]{3,2,1,0:T(8,128)(2,1)} %copy-done.2, bf16[2,2,80,320]{3,2,1,0:T(8,128)(2,1)} %copy-done.4, bf16[2,2,80,320]{3,2,1,0:T(8,128)(2,1)} %copy-done.3, bf16[2,2,80,320]{3,2,1,0:T(8,128)(2,1)} %copy-done.5), custom_call_target="tpu_custom_call" | custom-call | tf_op jit(solution)/shard_map/pallas_call | solution.py:297
  (57 shorter events, 11.2 us)
Async XLA Ops:
  0.6 4.8 %collective-permute-start = (f32[1,2,8]{2,1,0:T(2,128)}, f32[1,2,8]{2,1,0:T(2,128)S(1)}, u32[]{:S(2)}, u32[]{:S(2)}) collective-permute-start(f32[1,2,8]{2,1,0:T(2,128)} %bitcast.58), channel_id=1, source_target_pairs={{0,4},{4,0},{8,12},{12,8},{16,20},{20,16},{24,28},{28,24},{1,5},{5... | collective-permute-start | bytes 200 | tf_op jit(solution)/shard_map/ppermute | solution.py:403
  6.2 3.6 %collective-permute-start.1 = (f32[2,2,8]{2,1,0:T(2,128)S(1)}, f32[2,2,8]{2,1,0:T(2,128)S(1)}, u32[]{:S(2)}, u32[]{:S(2)}) collective-permute-start(f32[2,2,8]{2,1,0:T(2,128)S(1)} %maximum_select_fusion.2), channel_id=1, source_target_pairs={{0,8},{4,12},{8,0},{12,4},{16,24},{20,28},{24,16},{28,20},{1,9},{5... | collective-permute-start | bytes 392 | tf_op jit(solution)/shard_map/ppermute | solution.py:403
  9.9 4.6 %collective-permute-start.2 = (f32[4,2,8]{2,1,0:T(2,128)S(1)}, f32[4,2,8]{2,1,0:T(2,128)S(1)}, u32[]{:S(2)}, u32[]{:S(2)}) collective-permute-start(f32[4,2,8]{2,1,0:T(2,128)S(1)} %maximum_select_fusion.1), channel_id=1, source_target_pairs={{0,16},{4,20},{8,24},{12,28},{16,0},{20,4},{24,8},{28,12},{1,17},{... | collective-permute-start | bytes 776 | tf_op jit(solution)/shard_map/ppermute | solution.py:403
  14.5 0.6 copy-start.7
  17.1 0.8 copy-start
  34.7 5.2 %collective-permute-start.4 = (bf16[2,80,320]{2,1,0:T(8,128)(2,1)}, bf16[2,80,320]{2,1,0:T(8,128)(2,1)}, u32[]{:S(2)}, u32[]{:S(2)}) collective-permute-start(bf16[2,80,320]{2,1,0:T(8,128)(2,1)} %copy.61.refs_0_), channel_id=1, source_target_pairs={{0,2},{1,3},{2,0},{3,1},{4,6},{5,7},{6,4},{7,5},{8,10},{9,11},{10,... | collective-permute-start | bytes 307208 | tf_op jit(solution)/shard_map/ppermute | solution.py:403
  36.2 14.6 %collective-permute-start.3 = (bf16[2,80,320]{2,1,0:T(8,128)(2,1)}, bf16[2,80,320]{2,1,0:T(8,128)(2,1)}, u32[]{:S(2)}, u32[]{:S(2)}) collective-permute-start(bf16[2,80,320]{2,1,0:T(8,128)(2,1)} %copy.61.refs_0_), channel_id=1, source_target_pairs={{0,1},{1,0},{2,3},{3,2},{4,5},{5,4},{6,7},{7,6},{8,9},{9,8},{10,11... | collective-permute-start | bytes 307208 | tf_op jit(solution)/shard_map/ppermute | solution.py:403
  39.9 10.9 %collective-permute-start.5 = (bf16[2,80,320]{2,1,0:T(8,128)(2,1)}, bf16[2,80,320]{2,1,0:T(8,128)(2,1)}, u32[]{:S(2)}, u32[]{:S(2)}) collective-permute-start(bf16[2,80,320]{2,1,0:T(8,128)(2,1)} %collective-permute-done.4.refs_2_), channel_id=1, source_target_pairs={{0,1},{1,0},{2,3},{3,2},{4,5},{5,4},{6,7},{7,6},{8,9},{9,8},{10,11... | collective-permute-start | bytes 307208 | tf_op jit(solution)/shard_map/ppermute | solution.py:403
  48.7 18.4 %collective-permute-start.11 = (bf16[2,80,320]{2,1,0:T(8,128)(2,1)}, bf16[2,80,320]{2,1,0:T(8,128)(2,1)}, u32[]{:S(2)}, u32[]{:S(2)}) collective-permute-start(bf16[2,80,320]{2,1,0:T(8,128)(2,1)} %copy.71.refs_0_), channel_id=1, source_target_pairs={{0,3},{1,2},{2,1},{3,0},{4,7},{5,6},{6,5},{7,4},{8,11},{9,10},{10,... | collective-permute-start | bytes 307208 | tf_op jit(solution)/shard_map/ppermute | solution.py:403
  50.3 16.8 %collective-permute-start.10 = (bf16[2,80,320]{2,1,0:T(8,128)(2,1)}, bf16[2,80,320]{2,1,0:T(8,128)(2,1)}, u32[]{:S(2)}, u32[]{:S(2)}) collective-permute-start(bf16[2,80,320]{2,1,0:T(8,128)(2,1)} %copy.71.refs_0_), channel_id=1, source_target_pairs={{0,2},{1,3},{2,0},{3,1},{4,6},{5,7},{6,4},{7,5},{8,10},{9,11},{10,... | collective-permute-start | bytes 307208 | tf_op jit(solution)/shard_map/ppermute | solution.py:403
  50.8 16.3 %collective-permute-start.9 = (bf16[2,80,320]{2,1,0:T(8,128)(2,1)}, bf16[2,80,320]{2,1,0:T(8,128)(2,1)}, u32[]{:S(2)}, u32[]{:S(2)}) collective-permute-start(bf16[2,80,320]{2,1,0:T(8,128)(2,1)} %copy.71.refs_0_), channel_id=1, source_target_pairs={{0,1},{1,0},{2,3},{3,2},{4,5},{5,4},{6,7},{7,6},{8,9},{9,8},{10,11... | collective-permute-start | bytes 307208 | tf_op jit(solution)/shard_map/ppermute | solution.py:403
  87.4 19.8 %copy-start.6 = (f32[2,80,320]{2,1,0:T(8,128)S(1)}, f32[2,80,320]{2,1,0:T(8,128)}, u32[]{:S(2)}) copy-start(f32[2,80,320]{2,1,0:T(8,128)} %get-tuple-element.30) | copy-start | bytes 614404
  87.4 2.8 %collective-permute-start.13 = (f32[2,80,320]{2,1,0:T(8,128)}, f32[2,80,320]{2,1,0:T(8,128)S(1)}, u32[]{:S(2)}, u32[]{:S(2)}) collective-permute-start(f32[2,80,320]{2,1,0:T(8,128)} %get-tuple-element.33), channel_id=1, source_target_pairs={{0,1},{1,0},{2,3},{3,2},{4,5},{5,4},{6,7},{7,6},{8,9},{9,8},{10,11... | collective-permute-start | bytes 614408 | tf_op jit(solution)/shard_map/ppermute | solution.py:403
  87.9 4.8 %collective-permute-start.6 = (f32[2,80,320]{2,1,0:T(8,128)}, f32[2,80,320]{2,1,0:T(8,128)S(1)}, u32[]{:S(2)}, u32[]{:S(2)}) collective-permute-start(f32[2,80,320]{2,1,0:T(8,128)} %get-tuple-element.23), channel_id=1, source_target_pairs={{0,1},{1,0},{2,3},{3,2},{4,5},{5,4},{6,7},{7,6},{8,9},{9,8},{10,11... | collective-permute-start | bytes 614408 | tf_op jit(solution)/shard_map/ppermute | solution.py:403
  88.0 9.0 %collective-permute-start.7 = (f32[2,80,320]{2,1,0:T(8,128)}, f32[2,80,320]{2,1,0:T(8,128)S(1)}, u32[]{:S(2)}, u32[]{:S(2)}) collective-permute-start(f32[2,80,320]{2,1,0:T(8,128)} %get-tuple-element.24), channel_id=1, source_target_pairs={{0,2},{1,3},{2,0},{3,1},{4,6},{5,7},{6,4},{7,5},{8,10},{9,11},{10,... | collective-permute-start | bytes 614408 | tf_op jit(solution)/shard_map/ppermute | solution.py:403
  89.5 11.9 %collective-permute-start.8 = (f32[2,80,320]{2,1,0:T(8,128)}, f32[2,80,320]{2,1,0:T(8,128)S(1)}, u32[]{:S(2)}, u32[]{:S(2)}) collective-permute-start(f32[2,80,320]{2,1,0:T(8,128)} %get-tuple-element.25), channel_id=1, source_target_pairs={{0,3},{1,2},{2,1},{3,0},{4,7},{5,6},{6,5},{7,4},{8,11},{9,10},{10,... | collective-permute-start | bytes 614408 | tf_op jit(solution)/shard_map/ppermute | solution.py:403
  89.8 17.3 %collective-permute-start.12 = (f32[2,80,320]{2,1,0:T(8,128)}, f32[2,80,320]{2,1,0:T(8,128)S(1)}, u32[]{:S(2)}, u32[]{:S(2)}) collective-permute-start(f32[2,80,320]{2,1,0:T(8,128)} %get-tuple-element.31), channel_id=1, source_target_pairs={{0,1},{1,0},{2,3},{3,2},{4,5},{5,4},{6,7},{7,6},{8,9},{9,8},{10,11... | collective-permute-start | bytes 614408 | tf_op jit(solution)/shard_map/ppermute | solution.py:403
  91.1 16.0 %collective-permute-start.14 = (f32[2,80,320]{2,1,0:T(8,128)S(1)}, f32[2,80,320]{2,1,0:T(8,128)S(1)}, u32[]{:S(2)}, u32[]{:S(2)}) collective-permute-start(f32[2,80,320]{2,1,0:T(8,128)S(1)} %add.41), channel_id=1, source_target_pairs={{0,2},{1,3},{2,0},{3,1},{4,6},{5,7},{6,4},{7,5},{8,10},{9,11},{10,... | collective-permute-start | bytes 614408 | tf_op jit(solution)/shard_map/ppermute | solution.py:403
  102.5 19.4 %copy-start.8 = (f32[8,2,8]{2,1,0:T(2,128)S(1)}, f32[8,2,8]{2,1,0:T(2,128)}, u32[]{:S(2)}) copy-start(f32[8,2,8]{2,1,0:T(2,128)} %copy-done.7) | copy-start | bytes 1540
  103.3 29.1 %copy-start.1 = (f32[8,2,80,40]{2,3,1,0:T(8,128)S(1)}, f32[8,2,80,40]{2,3,1,0:T(8,128)}, u32[]{:S(2)}) copy-start(f32[8,2,80,40]{2,3,1,0:T(8,128)} %param.14) | copy-start | bytes 614404
  103.3 14.9 %all-to-all-start.1 = ((f32[1,2,80,320]{2,1,0,3:T(2,128)}), f32[1,2,80,320]{2,1,0,3:T(2,128)S(1)}, u32[]{:S(2)}, u32[]{:S(2)}) async-start(f32[1,2,80,320]{2,1,0,3:T(2,128)} %copy.62), calls=%async_computation.1 | async-start | bytes 655360 | tf_op jit(solution)/shard_map/all_to_all | solution.py:464
  118.3 14.2 %all-to-all-start.2 = ((f32[1,2,80,320]{2,1,0,3:T(2,128)}), f32[1,2,80,320]{2,1,0,3:T(2,128)S(1)}, u32[]{:S(2)}, u32[]{:S(2)}) async-start(f32[1,2,80,320]{2,1,0,3:T(2,128)} %copy.72), calls=%async_computation.2 | async-start | bytes 655360 | tf_op jit(solution)/shard_map/all_to_all | solution.py:464
  148.3 7.8 %copy-start.2 = (bf16[2,2,80,320]{3,2,1,0:T(8,128)(2,1)}, bf16[2,2,80,320]{3,2,1,0:T(8,128)(2,1)S(1)}, u32[]{:S(2)}) copy-start(bf16[2,2,80,320]{3,2,1,0:T(8,128)(2,1)S(1)} %copy.82.refs_0_) | copy-start | bytes 614404
  148.3 6.3 %collective-permute-start.16 = (bf16[2,2,80,320]{3,2,1,0:T(8,128)(2,1)S(1)}, bf16[2,2,80,320]{3,2,1,0:T(8,128)(2,1)S(1)}, u32[]{:S(2)}, u32[]{:S(2)}) collective-permute-start(bf16[2,2,80,320]{3,2,1,0:T(8,128)(2,1)S(1)} %copy.82.refs_0_), channel_id=1, source_target_pairs={{0,2},{1,3},{2,0},{3,1},{4,6},{5,7},{6,4},{7,5},{8,10},{9,11},{10,... | collective-permute-start | bytes 614408 | tf_op jit(solution)/shard_map/ppermute | solution.py:403
  149.9 5.5 %collective-permute-start.15 = (bf16[2,2,80,320]{3,2,1,0:T(8,128)(2,1)S(1)}, bf16[2,2,80,320]{3,2,1,0:T(8,128)(2,1)S(1)}, u32[]{:S(2)}, u32[]{:S(2)}) collective-permute-start(bf16[2,2,80,320]{3,2,1,0:T(8,128)(2,1)S(1)} %copy.82.refs_0_), channel_id=1, source_target_pairs={{0,1},{1,0},{2,3},{3,2},{4,5},{5,4},{6,7},{7,6},{8,9},{9,8},{10,11... | collective-permute-start | bytes 614408 | tf_op jit(solution)/shard_map/ppermute | solution.py:403
  154.5 1.5 copy-start.3
  154.5 1.5 collective-permute-start.17
  155.3 0.7 copy-start.4
  156.1 0.7 copy-start.5
where the time goes:
time: 160 us; the launch traced here: 159 us
  Pallas kernels  45.9 us (29%)
  waiting for transfers between devices  42.9 us (27%)
  blocking collectives  29.3 us (18%)
  starting transfers between devices  25.1 us (16%)
  local copies, waits for them, and re-layouts  8.82 us (6%)
  matrix products  3.33 us (2%)
  other arithmetic  2.81 us (2%)
    pallas_call x3, Pallas kernels, normal_call(): pl.pallas_call(functools.partial(normal_kernel, size, len(before), frame,...  36.5 us
    all_to_all x2, blocking collectives, send_images(): lax.all_to_all(images, 'frame', split_axis=0, concat_axis=3, tiled=True)  29.3 us
    ppermute x18, waiting for transfers between devices, exchange(): return lax.ppermute(value, axis, [(i, i ^ distance) for i in range(size)])  22.7 us
    all_to_all x2, waiting for transfers between devices, send_residual(): lax.all_to_all(value[None], 'frame', split_axis=3, concat_axis=0, tiled=T...  20.2 us
    ppermute x18, starting transfers between devices, exchange(): return lax.ppermute(value, axis, [(i, i ^ distance) for i in range(size)])  17.7 us
    all_to_all x2, starting transfers between devices, send_residual(): lax.all_to_all(value[None], 'frame', split_axis=3, concat_axis=0, tiled=T...  7.4 us
    pallas_call x1, Pallas kernels, prepare_call(): pl.pallas_call(prepare_kernel, grid=(frames,), out_shape=(jax.ShapeDtypeS...  7.06 us
  transfers between devices with their start and end apart: 20, of which 10 were waited for; matrix products, arithmetic and copies ran while one was open for 4% of the time, Pallas kernels for 15%

commit v1 on v0

--- a/solution.py
+++ b/solution.py
@@ -5,6 +5,7 @@
 from jax.experimental import pallas as pl
 from jax.experimental.pallas import tpu as pltpu
 
+STEP_SIZE = 0.15
 LANES = 128
 VMEM_BYTES = 67043328
 F32, BF16 = jnp.float32, jnp.bfloat16
@@ -56,13 +57,44 @@
     return jnp.dot(left, right, preferred_element_type=F32)
 
 
+def packing(count, width):
+    groups = LANES // width
+    lines = -(-2 * count // groups)
+    return groups, -(-lines // 8) * 8
+
+
+def pack(rows, width):
+    total, cols = rows.shape
+    groups, lines = packing(total // 2, width)
+    missing = groups * lines - total
+    if missing:
+        rows = jnp.concatenate([rows, jnp.zeros((missing, cols), rows.dtype)], 0)
+    rest = LANES - groups * width
+    packed = []
+    for at in range(0, cols, width):
+        pieces = [rows[g * lines : (g + 1) * lines, at : at + width] for g in range(groups)]
+        if rest:
+            pieces.append(jnp.zeros((lines, rest), rows.dtype))
+        packed.append(jnp.concatenate(pieces, 1))
+    return packed
+
+
+def unpack(packed, total, width):
+    groups, _ = packing(total // 2, width)
+    bands = [jnp.concatenate([p[:, g * width : (g + 1) * width] for p in packed], 1) for g in range(groups)]
+    return jnp.concatenate(bands, 0)[:total]
+
+
 def normal_kernel(size, extra, frame, first_coil, me_ref, *refs):
-    parts, refs = refs[:size], refs[size:]
+    parts_hbm, refs = refs[:size], refs[size:]
     sens_hbm, sig_hbm, dif_hbm, data_hbm, tcol_hbm, trow_hbm, tback_hbm, tlast_hbm, sig0_ref, rev_ref = refs[:10]
     before, refs = refs[10 : 10 + extra], refs[10 + extra :]
     blocks, refs = refs[:size], refs[size:]
     sens_ref, tcol_ref, trow_ref, sig_ref, dif_ref, tback_ref, tlast_ref, data_ref, sems = refs[:9]
-    img_n, img_s, xcat, mid, back, last, acc = refs[9:]
+    parts, img_n, img_s, xcat, mid, back, last, acc = refs[9:]
+    arrived = [pltpu.make_async_copy(parts_hbm[n].at[:, frame], parts.at[n], sems.at[8 + n]) for n in range(size)]
+    for copy in arrived:
+        copy.start()
     chosen = pl.ds(first_coil, sens_ref.shape[0])
     moved = [
         pltpu.make_async_copy(source, target, sems.at[n])
@@ -84,9 +116,12 @@
     def place(number):
         return pl.ds(pl.multiple_of((me_ref[0] ^ number) * count, count), count)
 
+    width = cols // parts.shape[1]
     for number in range(size):
+        arrived[number].wait()
+        block = unpack([parts[number, n].astype(F32) for n in range(cols // width)], 2 * count, width)
         for part in range(2):
-            img_n[part, place(number)] = parts[number][part]
+            img_n[part, place(number)] = block[part * count : (part + 1) * count].astype(BF16)
     for part in range(2):
         for top, value in enumerate((img_n[part, half:].astype(F32), dot(rev_ref[...], img_n[part, :half]))):
             here = slice(top * half, top * half + half)
@@ -239,9 +274,9 @@
         acc[part, half:] = above
         acc[part, :half] = turned
     for number in range(size):
-        for part in range(2):
-            value = acc[part, place(number)]
-            blocks[number][part] = value + before[number][part] if extra == size else value
+        block = jnp.concatenate([acc[part, place(number)] for part in range(2)], 0)
+        for n, value in enumerate(pack(block, width)):
+            blocks[number][n] = value + before[number][n] if extra == size else value
 
 
 def normal_call(frame, chosen, me, parts, sens, sig, dif, sig0, data, tables, before):
@@ -257,16 +292,18 @@
     like = lambda value: pltpu.VMEM(value.shape, value.dtype)
     one = lambda value: pltpu.VMEM(value.shape[1:], value.dtype)
     some = lambda value: pltpu.VMEM((coils,) + value.shape[1:], value.dtype)
+    packed = parts[0].shape[:1] + parts[0].shape[2:]
     flops = 2 * coils * 2 * 12 * rows * cols * spectral
 
     return pl.pallas_call(
         functools.partial(normal_kernel, size, len(before), frame, chosen[0]),
-        out_shape=[jax.ShapeDtypeStruct((2, rows // size, cols), F32)] * size,
-        in_specs=[pl.BlockSpec(memory_space=pltpu.SMEM)] + [held] * size + [away] * 8 + [held] * 2 + [held if len(before) == size else away] * len(before),
+        out_shape=[jax.ShapeDtypeStruct(packed, F32)] * size,
+        in_specs=[pl.BlockSpec(memory_space=pltpu.SMEM)] + [away] * (size + 8) + [held] * 2 + [held if len(before) == size else away] * len(before),
         out_specs=[held] * size,
         scratch_shapes=[
             some(sens), like(tcol), like(trow), one(sig), one(dif), like(tback), like(tlast), some(one(data)),
-            pltpu.SemaphoreType.DMA((8,)),
+            pltpu.SemaphoreType.DMA((8 + size,)),
+            pltpu.VMEM((size,) + packed, BF16),
             pltpu.VMEM((2, rows, cols), BF16),
             pltpu.VMEM((2, rows, wide), F32),
             pltpu.VMEM((4 * half, tcol.shape[0] * 3 // 4), BF16),
@@ -280,26 +317,123 @@
     )(me, *parts, sens, sig, dif, data, tcol, trow, tback, tlast, sig0, rev, *before)
 
 
-def place_kernel(me_ref, *refs):
-    size = len(refs) - 1
-    parts, out_ref = refs[:size], refs[size]
-    count = parts[0].shape[2]
-    for number in range(size):
-        for frame in range(out_ref.shape[0]):
+def place_kernel(numbers, extra, me_ref, *refs):
+    total = len(numbers)
+    parts_hbm, out_hbm = refs[:total], refs[total + extra]
+    parts, blocks, sems = refs[total + extra + 1 :]
+    _, devices, frames, _, _ = parts.shape
+    count = blocks.shape[3]
+    width = blocks.shape[4] // devices
+    arrived = [pltpu.make_async_copy(parts_hbm[n], parts.at[n], sems.at[n]) for n in range(total)]
+    for copy in arrived:
+        copy.start()
+    leaving = []
+    for n, number in enumerate(numbers):
+        arrived[n].wait()
+        for frame in range(frames):
+            block = unpack([parts[n, device, frame].astype(F32) for device in range(devices)], 2 * count, width)
             for part in range(2):
-                there = pl.ds(pl.multiple_of((me_ref[0] ^ number) * count, count), count)
-                out_ref[frame, part, there] = parts[number][frame, part]
-
-
-def place_call(me, parts):
-    frames, _, count, cols = parts[0].shape
+                blocks[n, frame, part] = block[part * count : (part + 1) * count].astype(BF16)
+        there = pl.ds(pl.multiple_of((me_ref[0] ^ number) * count, count), count)
+        leaving.append(pltpu.make_async_copy(blocks.at[n], out_hbm.at[:, :, there], sems.at[total + n]))
+        leaving[-1].start()
+    for copy in leaving:
+        copy.wait()
+
+
+def place_call(me, parts, size, count, width, before):
+    numbers = sorted(parts)
+    devices, frames = parts[numbers[0]].shape[:2]
+    away = pl.BlockSpec(memory_space=pl.ANY)
+    total = len(numbers)
+    return pl.pallas_call(
+        functools.partial(place_kernel, numbers, len(before)),
+        out_shape=jax.ShapeDtypeStruct((frames, 2, count * size, width * devices), BF16),
+        in_specs=[pl.BlockSpec(memory_space=pltpu.SMEM)] + [away] * (total + len(before)),
+        out_specs=away,
+        input_output_aliases={1 + total: 0} if before else {},
+        scratch_shapes=[
+            pltpu.VMEM((total,) + parts[numbers[0]].shape, BF16),
+            pltpu.VMEM((total, frames, 2, count, width * devices), BF16),
+            pltpu.SemaphoreType.DMA((2 * total,)),
+        ],
+        compiler_params=pltpu.CompilerParams(vmem_limit_bytes=VMEM_BYTES),
+        cost_estimate=pl.CostEstimate(flops=1 << 20, bytes_accessed=4 * 1024 * 1024, transcendentals=0),
+    )(me, *[parts[number] for number in numbers], *before)
+
+
+def pack_kernel(factor_ref, out_ref):
+    for rank in range(factor_ref.shape[0]):
+        rows = jnp.concatenate([factor_ref[rank, 0].T, factor_ref[rank, 1].T], 0)
+        out_ref[rank] = pack(rows, factor_ref.shape[2])[0]
+
+
+def pack_call(factors):
+    ranks, _, count, width = factors.shape
+    lines = packing(count, width)[1]
+    shape = jax.ShapeDtypeStruct((ranks, lines, LANES), F32)
+    return pl.pallas_call(pack_kernel, out_shape=shape)(factors.transpose(0, 1, 3, 2))
+
+
+def unpack_kernel(packed_ref, out_ref):
+    _, _, width, count = out_ref.shape
+    for rank in range(out_ref.shape[0]):
+        block = unpack([packed_ref[rank]], 2 * count, width)
+        out_ref[rank, 0], out_ref[rank, 1] = block[:count].T, block[count:].T
+
+
+def unpack_call(packed, shape):
+    turned = jax.ShapeDtypeStruct(shape[:2] + (shape[3], shape[2]), F32)
+    return pl.pallas_call(unpack_kernel, out_shape=turned)(packed).transpose(0, 1, 3, 2)
+
+
+def mix(temporal_ref, factors, images_ref):
+    devices, frames, ranks = temporal_ref.shape
+    for device in range(devices):
+        for frame in range(frames):
+            value = temporal_ref[device, frame, 0] * factors[0]
+            for rank in range(1, ranks):
+                value = value + temporal_ref[device, frame, rank] * factors[rank]
+            images_ref[device, frame] = value.astype(BF16)
+
+
+def images_kernel(temporal_ref, factor_ref, images_ref):
+    mix(temporal_ref, [factor_ref[rank] for rank in range(factor_ref.shape[0])], images_ref)
+
+
+def update_kernel(temporal_ref, factor_ref, residual_ref, next_ref, images_ref):
+    devices, frames, ranks = temporal_ref.shape
+    factors = []
+    for rank in range(ranks):
+        gradient = 0.0
+        for frame in range(frames):
+            for device in range(devices):
+                gradient = gradient + temporal_ref[device, frame, rank] * residual_ref[device, frame]
+        factors.append(factor_ref[rank] - STEP_SIZE * gradient)
+        next_ref[rank] = factors[rank]
+    mix(temporal_ref, factors, images_ref)
+
+
+def images_call(temporal_all, packed):
+    devices, frames, _ = temporal_all.shape
+    return pl.pallas_call(
+        images_kernel,
+        out_shape=jax.ShapeDtypeStruct((devices, frames) + packed.shape[1:], BF16),
+        in_specs=[pl.BlockSpec(memory_space=pltpu.SMEM), pl.BlockSpec(memory_space=pltpu.VMEM)],
+    )(temporal_all, packed)
+
+
+def update_call(temporal_all, packed, residual):
+    devices, frames, _ = temporal_all.shape
     held = pl.BlockSpec(memory_space=pltpu.VMEM)
     return pl.pallas_call(
-        place_kernel,
-        out_shape=jax.ShapeDtypeStruct((frames, 2, count * len(parts), cols), parts[0].dtype),
-        in_specs=[pl.BlockSpec(memory_space=pltpu.SMEM)] + [held] * len(parts),
-        out_specs=held,
-    )(me, *parts)
+        update_kernel,
+        out_shape=(
+            jax.ShapeDtypeStruct(packed.shape, F32),
+            jax.ShapeDtypeStruct((devices, frames) + packed.shape[1:], BF16),
+        ),
+        in_specs=[pl.BlockSpec(memory_space=pltpu.SMEM)] + [held] * 2,
+    )(temporal_all, packed, residual)
 
 
 def freq_order_rows(rows, period):
@@ -375,9 +509,6 @@
     )(index, level, sens, row, col, rev, dup, after)
 
 
-STEP_SIZE = 0.15
-
-
 def one_hot(order):
     return (order[:, None] == np.arange(len(order))[None, :]).astype(BF16)
 
@@ -410,11 +541,7 @@
         for key in list(held):
             held[key ^ distance] = exchange(held[key], axis, distance)
         distance //= 2
-    return [held[key] for key in sorted(held)]
-
-
-def gather_direct(own, axis):
-    return [own] + [exchange(own, axis, distance) for distance in range(1, lax.axis_size(axis))]
+    return held
 
 
 def scatter_blocks(blocks, axis):
@@ -450,50 +577,42 @@
     return held
 
 
-def make_images(factors, temporal_all):
-    mixed = jnp.einsum("ftr,rcxy->ftcxy", temporal_all, factors, precision=lax.Precision.HIGHEST)
-    return mixed.astype(BF16)
-
-
-def send_images(images):
-    images = images.reshape((-1,) + images.shape[2:])
-    return lax.all_to_all(images, "frame", split_axis=0, concat_axis=3, tiled=True)
-
-
-def send_residual(value):
-    return lax.all_to_all(value[None], "frame", split_axis=3, concat_axis=0, tiled=True)
+def swap(value):
+    return lax.all_to_all(value, "frame", split_axis=0, concat_axis=0, tiled=True)
 
 
 def body(spatial, temporal, sensitivity, coil_data, kernel_index, kernel_level):
     rows, cols = sensitivity.shape[2:]
     tables, perms = constants(rows, cols, kernel_index.shape[1], kernel_index.shape[2])
     me = lax.axis_index("coil").astype(jnp.int32)[None]
+    size = lax.axis_size("coil")
     temporal_all = gather_small(temporal, "frame")
-    images = make_images(spatial, temporal_all)
-    own = send_images(images)
-    frames = own.shape[0]
+    packed = pack_call(spatial)
+    images = images_call(temporal_all, packed)
+    own = swap(images)
+    frames = own.shape[1]
 
     sig, dif, sig0, wide = prepare_call(kernel_index, kernel_level, sensitivity, perms, images)
+    held = gather_blocks(own, "coil")
+    parts = [held[number] for number in range(size)]
     blocks = []
-    coils = list(range(sensitivity.shape[0]))
+    coils = range(sensitivity.shape[0])
     for frame in range(frames):
-        parts = (gather_direct if frame else gather_blocks)(own[frame], "coil")
-        groups = [coils[:1], coils[1:]] if frame and len(coils) > 1 else [coils]
         before = blocks[-1][:1] if blocks else []
-        for group in groups:
-            before = normal_call(frame, group, me, parts, wide, sig, dif, sig0, coil_data, tables, before)
-        blocks.append(before)
-    gradient = 0.0
+        blocks.append(normal_call(frame, coils, me, parts, wide, sig, dif, sig0, coil_data, tables, before))
+    sums = []
     for frame in range(frames):
-        final = frame == frames - 1
-        rows_sum = (scatter_blocks if final else scatter_direct)(blocks[frame], "coil")
-        residual = send_residual(rows_sum)
-        gradient = gradient + jnp.einsum(
-            "fr,fcxy->rcxy", temporal_all[:, frame], residual, precision=lax.Precision.HIGHEST
-        )
-    spatial_next = spatial - STEP_SIZE * gradient
-    parts = gather_blocks(send_images(make_images(spatial_next, temporal_all)), "coil")
-    return spatial_next, place_call(me, parts)
+        sums.append((scatter_blocks if frame == frames - 1 else scatter_direct)(blocks[frame], "coil"))
+    residual = swap(jnp.stack(sums, 1))
+    packed_next, images = update_call(temporal_all, packed, residual)
+    own = swap(images)
+    spatial_next = unpack_call(packed_next, spatial.shape)
+    held = gather_blocks(own, "coil")
+    out = []
+    for chosen in (range(size // 2), range(size // 2, size)):
+        group = {number: held[number] for number in chosen}
+        out = [place_call(me, group, size, spatial.shape[2], spatial.shape[3], out)]
+    return spatial_next, out[0]
 
 
 def solution(mesh):

time: 160 us -> 142 us (0.89)
  waiting for transfers between devices: 42.9 us -> 25.1 us
  blocking collectives: 29.3 us -> 41.8 us
  starting transfers between devices: 25.1 us -> 15.5 us
  local copies, waits for them, and re-layouts: 8.82 us -> 0.01 us
  Pallas kernels: 45.9 us -> 54.2 us
  matrix products: 3.33 us -> 0 us
    all_to_all x2 -> x0, waiting for transfers between devices: 20.2 us -> none  [send_residual(): lax.all_to_all(value[None], 'frame', split_axis=3, concat_axis=0, tiled=T...]
    all_to_all x2 -> x3, blocking collectives: 29.3 us -> 41.8 us  [swap(): lax.all_to_all(value, 'frame', split_axis=0, concat_axis=0, tiled=True)]
    pallas_call x1 -> x6, Pallas kernels: 2.34 us -> 12.6 us  [the longest x2 4.22 us: place_call(): pl.pallas_call(functools.partial(place_kernel, numbers, len(before)), out...]
    all_to_all x2 -> x0, starting transfers between devices: 7.4 us -> none  [send_residual(): lax.all_to_all(value[None], 'frame', split_axis=3, concat_axis=0, tiled=T...]
    dot_general x4 -> x0, matrix products: 3.33 us -> none  [the longest x2 2.3 us: make_images(): jnp.einsum('ftr,rcxy->ftcxy', temporal_all, factors, precision=lax.Precis...]
    unnamed x19 -> x4, local copies, waits for them, and re-layouts: 2.95 us -> 0.01 us
    ppermute x18 -> x15, waiting for transfers between devices: 22.7 us -> 25.1 us  [exchange(): return lax.ppermute(value, axis, [(i, i ^ distance) for i in range(size)])]
    ppermute x18 -> x15, starting transfers between devices: 17.7 us -> 15.5 us  [exchange(): return lax.ppermute(value, axis, [(i, i ^ distance) for i in range(size)])]
  transfers between devices with their start and end apart: 20 -> 15, of which waited for: 10 -> 7; matrix products, arithmetic and copies ran while one was open for 4% -> 1% of each run, Pallas kernels for 15% -> 9%
where the time goes in v1:
time: 142 us; the launch traced here: 141 us
  Pallas kernels  54.2 us (38%)
  blocking collectives  41.8 us (29%)
  waiting for transfers between devices  25.1 us (18%)
  starting transfers between devices  15.5 us (11%)
  other arithmetic  3.39 us (2%)
    all_to_all x3, blocking collectives, swap(): lax.all_to_all(value, 'frame', split_axis=0, concat_axis=0, tiled=True)  41.8 us
    pallas_call x2, Pallas kernels, normal_call(): pl.pallas_call(functools.partial(normal_kernel, size, len(before), frame,...  34.6 us
    ppermute x15, waiting for transfers between devices, exchange(): return lax.ppermute(value, axis, [(i, i ^ distance) for i in range(size)])  25.1 us
    ppermute x15, starting transfers between devices, exchange(): return lax.ppermute(value, axis, [(i, i ^ distance) for i in range(size)])  15.5 us
    pallas_call x1, Pallas kernels, prepare_call(): pl.pallas_call(prepare_kernel, grid=(frames,), out_shape=(jax.ShapeDtypeS...  7.05 us
    pallas_call x2, Pallas kernels, place_call(): pl.pallas_call(functools.partial(place_kernel, numbers, len(before)), out...  4.22 us
  transfers between devices with their start and end apart: 15, of which 7 were waited for; matrix products, arithmetic and copies ran while one was open for 1% of the time, Pallas kernels for 9%

profile of v1, /device:TPU:0, one launch (start us, length us, event | category | flops | bytes accessed | tf_op | source)
XLA Modules:
  0.0 140.9 jit_solution(18186555867600650211)
XLA Ops:
  0.6 3.1 %collective-permute-start = (f32[1,2,8]{2,1,0:T(2,128)}, f32[1,2,8]{2,1,0:T(2,128)S(1)}, u32[]{:S(2)}, u32[]{:S(2)}) collective-permute-start(f32[1,2,8]{2,1,0:T(2,128)} %bitcast.10), channel_id=1, source_target_pairs={{0,4},{4,0},{8,12},{12,8},{16,20},{20,16},{24,28},{28,24},{1,5},{5... | collective-permute-start | bytes 200 | tf_op jit(solution)/shard_map/ppermute | solution.py:534
  3.7 1.8 %collective-permute-done = f32[1,2,8]{2,1,0:T(2,128)S(1)} collective-permute-done((f32[1,2,8]{2,1,0:T(2,128)}, f32[1,2,8]{2,1,0:T(2,128)S(1)}, u32[]{:S(2)}, u32[]{:S(2)}) %collective-permute-start) | collective-permute-done | bytes 96 | tf_op jit(solution)/shard_map/ppermute | solution.py:534
  5.5 0.8 maximum_select_fusion.2
  6.2 2.1 %collective-permute-start.1 = (f32[2,2,8]{2,1,0:T(2,128)S(1)}, f32[2,2,8]{2,1,0:T(2,128)S(1)}, u32[]{:S(2)}, u32[]{:S(2)}) collective-permute-start(f32[2,2,8]{2,1,0:T(2,128)S(1)} %maximum_select_fusion.2), channel_id=1, source_target_pairs={{0,8},{4,12},{8,0},{12,4},{16,24},{20,28},{24,16},{28,20},{1,9},{5... | collective-permute-start | bytes 392 | tf_op jit(solution)/shard_map/ppermute | solution.py:534
  8.3 1.6 %collective-permute-done.1 = f32[2,2,8]{2,1,0:T(2,128)S(1)} collective-permute-done((f32[2,2,8]{2,1,0:T(2,128)S(1)}, f32[2,2,8]{2,1,0:T(2,128)S(1)}, u32[]{:S(2)}, u32[]{:S(2)}) %collective-permute-start.1) | collective-permute-done | bytes 160 | tf_op jit(solution)/shard_map/ppermute | solution.py:534
  9.9 3.0 %collective-permute-start.2 = (f32[4,2,8]{2,1,0:T(2,128)S(1)}, f32[4,2,8]{2,1,0:T(2,128)S(1)}, u32[]{:S(2)}, u32[]{:S(2)}) collective-permute-start(f32[4,2,8]{2,1,0:T(2,128)S(1)} %maximum_select_fusion.1), channel_id=1, source_target_pairs={{0,16},{4,20},{8,24},{12,28},{16,0},{20,4},{24,8},{28,12},{1,17},{... | collective-permute-start | bytes 776 | tf_op jit(solution)/shard_map/ppermute | solution.py:534
  12.9 2.0 %shard_map.149.factor_ref = f32[8,56,128]{2,1,0:T(8,128)} custom-call(f32[8,2,40,80]{3,2,1,0:T(8,128)} %bitcast.8), custom_call_target="tpu_custom_call" | custom-call | tf_op jit(solution)/shard_map/pallas_call | solution.py:375
  14.9 0.6 maximum_select_fusion.temporal_ref
  15.5 1.9 %shard_map.150.after_ref = bf16[8,2,56,128]{3,2,1,0:T(8,128)(2,1)} custom-call(f32[8,2,8]{2,1,0:T(2,128)} %maximum_select_fusion.temporal_ref, f32[8,56,128]{2,1,0:T(8,128)} %shard_map.149.factor_ref), custom_call_target="tpu_custom_call" | custom-call | tf_op jit(solution)/shard_map/pallas_call | solution.py:419
  17.4 13.8 %all_to_all.15.refs_0_ = bf16[8,2,56,128]{3,2,1,0:T(8,128)(2,1)} all-to-all(bf16[8,2,56,128]{3,2,1,0:T(8,128)(2,1)} %shard_map.150.after_ref), channel_id=1, replica_groups=mesh['frame'=8,'coil'=4] {'frame'}, dimensions={0} | all-to-all | bytes 458752 | tf_op jit(solution)/shard_map/all_to_all | solution.py:581
  31.2 1.5 %collective-permute-start.4 = (bf16[8,2,56,128]{3,2,1,0:T(8,128)(2,1)}, bf16[8,2,56,128]{3,2,1,0:T(8,128)(2,1)}, u32[]{:S(2)}, u32[]{:S(2)}) collective-permute-start(bf16[8,2,56,128]{3,2,1,0:T(8,128)(2,1)} %all_to_all.15.refs_0_), channel_id=1, source_target_pairs={{0,2},{1,3},{2,0},{3,1},{4,6},{5,7},{6,4},{7,5},{8,10},{9,11},{10,... | collective-permute-start | bytes 688136 | tf_op jit(solution)/shard_map/ppermute | solution.py:534
  32.7 4.8 %collective-permute-done.4.refs_2_ = bf16[8,2,56,128]{3,2,1,0:T(8,128)(2,1)} collective-permute-done((bf16[8,2,56,128]{3,2,1,0:T(8,128)(2,1)}, bf16[8,2,56,128]{3,2,1,0:T(8,128)(2,1)}, u32[]{:S(2)}, u32[]{:S(2)}) %collective-permute-start.4) | collective-permute-done | bytes 229408 | tf_op jit(solution)/shard_map/ppermute | solution.py:534
  37.6 7.1 %shard_map.151 = (f32[2,320,640]{2,1,0:T(8,128)}, f32[2,320,640]{2,1,0:T(8,128)}, f32[2,8,640]{2,1,0:T(8,128)}, bf16[2,2,320,384]{3,2,1,0:T(8,128)(2,1)}) custom-call(s32[2,640,640]{2,1,0:T(8,128)} %index_ref.1, f32[2,8]{1,0:T(2,128)} %level_ref.1, bf16[2,2,320,320]{3,2,1,0:T(8,128)(2,1)} %sens_ref.1, bf16[320,320]{1,0:T(8,128)(2,1)} %constant.81.clone.row_ref, ...), custom_call_target="tpu_custom_call" | custom-call | flops 1572864000 | bytes 16777216 | tf_op jit(solution)/shard_map/pallas_call | solution.py:487
  44.7 17.2 %shard_map.152 = (f32[8,56,128]{2,1,0:T(8,128)}, f32[8,56,128]{2,1,0:T(8,128)}, f32[8,56,128]{2,1,0:T(8,128)}, f32[8,56,128]{2,1,0:T(8,128)}) custom-call(s32[1]{0:T(128)} %bitcast.2.me_ref, bf16[8,2,56,128]{3,2,1,0:T(8,128)(2,1)} %all_to_all.15.refs_0_, bf16[8,2,56,128]{3,2,1,0:T(8,128)(2,1)} %collective-permute-done.3.refs_1_, ...), custom_call_target="tpu_custom_call" | custom-call | flops 6291456000 | bytes 8388608 | tf_op jit(solution)/shard_map/pallas_call | solution.py:298
  61.8 17.4 %shard_map.153 = (f32[8,56,128]{2,1,0:T(8,128)}, f32[8,56,128]{2,1,0:T(8,128)}, f32[8,56,128]{2,1,0:T(8,128)}, f32[8,56,128]{2,1,0:T(8,128)}) custom-call(s32[1]{0:T(128)} %bitcast.2.me_ref, bf16[8,2,56,128]{3,2,1,0:T(8,128)(2,1)} %all_to_all.15.refs_0_, bf16[8,2,56,128]{3,2,1,0:T(8,128)(2,1)} %collective-permute-done.3.refs_1_, ...), custom_call_target="tpu_custom_call" | custom-call | flops 6291456000 | bytes 8388608 | tf_op jit(solution)/shard_map/pallas_call | solution.py:298
  79.2 0.6 collective-permute-start.10
  79.9 1.5 %collective-permute-start.7 = (f32[8,56,128]{2,1,0:T(8,128)}, f32[8,56,128]{2,1,0:T(8,128)S(1)}, u32[]{:S(2)}, u32[]{:S(2)}) collective-permute-start(f32[8,56,128]{2,1,0:T(8,128)} %get-tuple-element.22), channel_id=1, source_target_pairs={{0,2},{1,3},{2,0},{3,1},{4,6},{5,7},{6,4},{7,5},{8,10},{9,11},{10,... | collective-permute-start | bytes 688136 | tf_op jit(solution)/shard_map/ppermute | solution.py:534
  81.7 0.4 collective-permute-start.9
  82.0 1.0 add.38
  83.0 1.6 %collective-permute-start.11 = (f32[8,56,128]{2,1,0:T(8,128)S(1)}, f32[8,56,128]{2,1,0:T(8,128)S(1)}, u32[]{:S(2)}, u32[]{:S(2)}) collective-permute-start(f32[8,56,128]{2,1,0:T(8,128)S(1)} %add.38), channel_id=1, source_target_pairs={{0,2},{1,3},{2,0},{3,1},{4,6},{5,7},{6,4},{7,5},{8,10},{9,11},{10,... | collective-permute-start | bytes 688136 | tf_op jit(solution)/shard_map/ppermute | solution.py:534
  84.6 4.0 %collective-permute-done.7 = f32[8,56,128]{2,1,0:T(8,128)S(1)} collective-permute-done((f32[8,56,128]{2,1,0:T(8,128)}, f32[8,56,128]{2,1,0:T(8,128)S(1)}, u32[]{:S(2)}, u32[]{:S(2)}) %collective-permute-start.7) | collective-permute-done | bytes 229408 | tf_op jit(solution)/shard_map/ppermute | solution.py:534
  88.6 4.0 %collective-permute-done.8 = f32[8,56,128]{2,1,0:T(8,128)S(1)} collective-permute-done((f32[8,56,128]{2,1,0:T(8,128)}, f32[8,56,128]{2,1,0:T(8,128)S(1)}, u32[]{:S(2)}, u32[]{:S(2)}) %collective-permute-start.8) | collective-permute-done | bytes 229408 | tf_op jit(solution)/shard_map/ppermute | solution.py:534
  92.6 1.0 add_bitcast_fusion.1
  93.6 4.3 %collective-permute-done.11 = f32[8,56,128]{2,1,0:T(8,128)S(1)} collective-permute-done((f32[8,56,128]{2,1,0:T(8,128)S(1)}, f32[8,56,128]{2,1,0:T(8,128)S(1)}, u32[]{:S(2)}, u32[]{:S(2)}) %collective-permute-start.11) | collective-permute-done | bytes 229408 | tf_op jit(solution)/shard_map/ppermute | solution.py:534
  97.9 16.3 %all_to_all.16.residual_ref = f32[8,2,56,128]{3,2,1,0:T(8,128)} all-to-all(f32[8,2,56,128]{3,2,1,0:T(8,128)S(1)} %pad_maximum_fusion), channel_id=1, replica_groups=mesh['frame'=8,'coil'=4] {'frame'}, dimensions={0} | all-to-all | bytes 917504 | tf_op jit(solution)/shard_map/all_to_all | solution.py:581
  114.2 2.4 %shard_map.154 = (f32[8,56,128]{2,1,0:T(8,128)}, bf16[8,2,56,128]{3,2,1,0:T(8,128)(2,1)}) custom-call(f32[8,2,8]{2,1,0:T(2,128)} %maximum_select_fusion.temporal_ref, f32[8,56,128]{2,1,0:T(8,128)} %shard_map.149.factor_ref, f32[8,2,56,128]{3,2,1,0:T(8,128)} %all_to_all.16.residual_ref), custom_call_target="tpu_custom_call" | custom-call | tf_op jit(solution)/shard_map/pallas_call | solution.py:429
  116.6 11.7 %all_to_all.17.refs_0_ = bf16[8,2,56,128]{3,2,1,0:T(8,128)(2,1)S(1)} all-to-all(bf16[8,2,56,128]{3,2,1,0:T(8,128)(2,1)} %get-tuple-element.29), channel_id=1, replica_groups=mesh['frame'=8,'coil'=4] {'frame'}, dimensions={0} | all-to-all | bytes 458752 | tf_op jit(solution)/shard_map/all_to_all | solution.py:581
  128.3 1.5 %collective-permute-start.12 = (bf16[8,2,56,128]{3,2,1,0:T(8,128)(2,1)S(1)}, bf16[8,2,56,128]{3,2,1,0:T(8,128)(2,1)}, u32[]{:S(2)}, u32[]{:S(2)}) collective-permute-start(bf16[8,2,56,128]{3,2,1,0:T(8,128)(2,1)S(1)} %all_to_all.17.refs_0_), channel_id=1, source_target_pairs={{0,2},{1,3},{2,0},{3,1},{4,6},{5,7},{6,4},{7,5},{8,10},{9,11},{10,... | collective-permute-start | bytes 688136 | tf_op jit(solution)/shard_map/ppermute | solution.py:534
  129.8 4.6 %collective-permute-done.12.refs_0_ = bf16[8,2,56,128]{3,2,1,0:T(8,128)(2,1)} collective-permute-done((bf16[8,2,56,128]{3,2,1,0:T(8,128)(2,1)S(1)}, bf16[8,2,56,128]{3,2,1,0:T(8,128)(2,1)}, u32[]{:S(2)}, u32[]{:S(2)}) %collective-permute-start.12) | collective-permute-done | bytes 229408 | tf_op jit(solution)/shard_map/ppermute | solution.py:534
  134.5 2.0 %shard_map.155 = f32[8,2,40,80]{3,2,1,0:T(8,128)} custom-call(f32[8,56,128]{2,1,0:T(8,128)} %get-tuple-element.28.packed_ref), custom_call_target="tpu_custom_call" | custom-call | tf_op jit(solution)/shard_map/pallas_call | solution.py:387
  136.5 2.1 %shard_map.156.refs_2_ = bf16[2,2,320,320]{3,2,1,0:T(8,128)(2,1)} custom-call(s32[1]{0:T(128)} %bitcast.2.me_ref, bf16[8,2,56,128]{3,2,1,0:T(8,128)(2,1)} %copy-done, bf16[8,2,56,128]{3,2,1,0:T(8,128)(2,1)} %collective-permute-done.14.refs_1_), custom_call_target="tpu_custom_call" | custom-call | flops 1048576 | bytes 4194304 | tf_op jit(solution)/shard_map/pallas_call | solution.py:349
  138.6 2.1 %shard_map.157 = bf16[2,2,320,320]{3,2,1,0:T(8,128)(2,1)} custom-call(s32[1]{0:T(128)} %bitcast.2.me_ref, bf16[8,2,56,128]{3,2,1,0:T(8,128)(2,1)} %collective-permute-done.12.refs_0_, bf16[8,2,56,128]{3,2,1,0:T(8,128)(2,1)} %collective-permute-done.13.refs_1_, bf16[2,2,320,320]{3,2,1,0:T(8,128)(2,1)} %shard_map.156.refs_2_), custom_call_target="tpu_custom_call", output_to_operand_aliasing={{}: (3, {})} | custom-call | flops 1048576 | bytes 4194304 | tf_op jit(solution)/shard_map/pallas_call | solution.py:349
  (21 shorter events, 0.5 us)
Async XLA Ops:
  0.6 4.8 %collective-permute-start = (f32[1,2,8]{2,1,0:T(2,128)}, f32[1,2,8]{2,1,0:T(2,128)S(1)}, u32[]{:S(2)}, u32[]{:S(2)}) collective-permute-start(f32[1,2,8]{2,1,0:T(2,128)} %bitcast.10), channel_id=1, source_target_pairs={{0,4},{4,0},{8,12},{12,8},{16,20},{20,16},{24,28},{28,24},{1,5},{5... | collective-permute-start | bytes 200 | tf_op jit(solution)/shard_map/ppermute | solution.py:534
  6.2 3.6 %collective-permute-start.1 = (f32[2,2,8]{2,1,0:T(2,128)S(1)}, f32[2,2,8]{2,1,0:T(2,128)S(1)}, u32[]{:S(2)}, u32[]{:S(2)}) collective-permute-start(f32[2,2,8]{2,1,0:T(2,128)S(1)} %maximum_select_fusion.2), channel_id=1, source_target_pairs={{0,8},{4,12},{8,0},{12,4},{16,24},{20,28},{24,16},{28,20},{1,9},{5... | collective-permute-start | bytes 392 | tf_op jit(solution)/shard_map/ppermute | solution.py:534
  9.9 5.1 %collective-permute-start.2 = (f32[4,2,8]{2,1,0:T(2,128)S(1)}, f32[4,2,8]{2,1,0:T(2,128)S(1)}, u32[]{:S(2)}, u32[]{:S(2)}) collective-permute-start(f32[4,2,8]{2,1,0:T(2,128)S(1)} %maximum_select_fusion.1), channel_id=1, source_target_pairs={{0,16},{4,20},{8,24},{12,28},{16,0},{20,4},{24,8},{28,12},{1,17},{... | collective-permute-start | bytes 776 | tf_op jit(solution)/shard_map/ppermute | solution.py:534
  31.2 6.3 %collective-permute-start.4 = (bf16[8,2,56,128]{3,2,1,0:T(8,128)(2,1)}, bf16[8,2,56,128]{3,2,1,0:T(8,128)(2,1)}, u32[]{:S(2)}, u32[]{:S(2)}) collective-permute-start(bf16[8,2,56,128]{3,2,1,0:T(8,128)(2,1)} %all_to_all.15.refs_0_), channel_id=1, source_target_pairs={{0,2},{1,3},{2,0},{3,1},{4,6},{5,7},{6,4},{7,5},{8,10},{9,11},{10,... | collective-permute-start | bytes 688136 | tf_op jit(solution)/shard_map/ppermute | solution.py:534
  32.7 11.9 %collective-permute-start.3 = (bf16[8,2,56,128]{3,2,1,0:T(8,128)(2,1)}, bf16[8,2,56,128]{3,2,1,0:T(8,128)(2,1)}, u32[]{:S(2)}, u32[]{:S(2)}) collective-permute-start(bf16[8,2,56,128]{3,2,1,0:T(8,128)(2,1)} %all_to_all.15.refs_0_), channel_id=1, source_target_pairs={{0,1},{1,0},{2,3},{3,2},{4,5},{5,4},{6,7},{7,6},{8,9},{9,8},{10,11... | collective-permute-start | bytes 688136 | tf_op jit(solution)/shard_map/ppermute | solution.py:534
  37.6 7.1 %collective-permute-start.5 = (bf16[8,2,56,128]{3,2,1,0:T(8,128)(2,1)}, bf16[8,2,56,128]{3,2,1,0:T(8,128)(2,1)}, u32[]{:S(2)}, u32[]{:S(2)}) collective-permute-start(bf16[8,2,56,128]{3,2,1,0:T(8,128)(2,1)} %collective-permute-done.4.refs_2_), channel_id=1, source_target_pairs={{0,1},{1,0},{2,3},{3,2},{4,5},{5,4},{6,7},{7,6},{8,9},{9,8},{10,11... | collective-permute-start | bytes 688136 | tf_op jit(solution)/shard_map/ppermute | solution.py:534
  79.2 18.6 %copy-start.1 = (f32[8,56,128]{2,1,0:T(8,128)S(1)}, f32[8,56,128]{2,1,0:T(8,128)}, u32[]{:S(2)}) copy-start(f32[8,56,128]{2,1,0:T(8,128)} %get-tuple-element.24) | copy-start | bytes 688132
  79.2 2.8 %collective-permute-start.10 = (f32[8,56,128]{2,1,0:T(8,128)}, f32[8,56,128]{2,1,0:T(8,128)S(1)}, u32[]{:S(2)}, u32[]{:S(2)}) collective-permute-start(f32[8,56,128]{2,1,0:T(8,128)} %get-tuple-element.27), channel_id=1, source_target_pairs={{0,1},{1,0},{2,3},{3,2},{4,5},{5,4},{6,7},{7,6},{8,9},{9,8},{10,11... | collective-permute-start | bytes 688136 | tf_op jit(solution)/shard_map/ppermute | solution.py:534
  79.8 4.7 %collective-permute-start.6 = (f32[8,56,128]{2,1,0:T(8,128)}, f32[8,56,128]{2,1,0:T(8,128)S(1)}, u32[]{:S(2)}, u32[]{:S(2)}) collective-permute-start(f32[8,56,128]{2,1,0:T(8,128)} %get-tuple-element.21), channel_id=1, source_target_pairs={{0,1},{1,0},{2,3},{3,2},{4,5},{5,4},{6,7},{7,6},{8,9},{9,8},{10,11... | collective-permute-start | bytes 688136 | tf_op jit(solution)/shard_map/ppermute | solution.py:534
  79.9 8.7 %collective-permute-start.7 = (f32[8,56,128]{2,1,0:T(8,128)}, f32[8,56,128]{2,1,0:T(8,128)S(1)}, u32[]{:S(2)}, u32[]{:S(2)}) collective-permute-start(f32[8,56,128]{2,1,0:T(8,128)} %get-tuple-element.22), channel_id=1, source_target_pairs={{0,2},{1,3},{2,0},{3,1},{4,6},{5,7},{6,4},{7,5},{8,10},{9,11},{10,... | collective-permute-start | bytes 688136 | tf_op jit(solution)/shard_map/ppermute | solution.py:534
  81.4 11.2 %collective-permute-start.8 = (f32[8,56,128]{2,1,0:T(8,128)}, f32[8,56,128]{2,1,0:T(8,128)S(1)}, u32[]{:S(2)}, u32[]{:S(2)}) collective-permute-start(f32[8,56,128]{2,1,0:T(8,128)} %get-tuple-element.23), channel_id=1, source_target_pairs={{0,3},{1,2},{2,1},{3,0},{4,7},{5,6},{6,5},{7,4},{8,11},{9,10},{10,... | collective-permute-start | bytes 688136 | tf_op jit(solution)/shard_map/ppermute | solution.py:534
  81.7 11.9 %collective-permute-start.9 = (f32[8,56,128]{2,1,0:T(8,128)}, f32[8,56,128]{2,1,0:T(8,128)S(1)}, u32[]{:S(2)}, u32[]{:S(2)}) collective-permute-start(f32[8,56,128]{2,1,0:T(8,128)} %get-tuple-element.25), channel_id=1, source_target_pairs={{0,1},{1,0},{2,3},{3,2},{4,5},{5,4},{6,7},{7,6},{8,9},{9,8},{10,11... | collective-permute-start | bytes 688136 | tf_op jit(solution)/shard_map/ppermute | solution.py:534
  83.0 14.9 %collective-permute-start.11 = (f32[8,56,128]{2,1,0:T(8,128)S(1)}, f32[8,56,128]{2,1,0:T(8,128)S(1)}, u32[]{:S(2)}, u32[]{:S(2)}) collective-permute-start(f32[8,56,128]{2,1,0:T(8,128)S(1)} %add.38), channel_id=1, source_target_pairs={{0,2},{1,3},{2,0},{3,1},{4,6},{5,7},{6,4},{7,5},{8,10},{9,11},{10,... | collective-permute-start | bytes 688136 | tf_op jit(solution)/shard_map/ppermute | solution.py:534
  128.3 1.5 %copy-start = (bf16[8,2,56,128]{3,2,1,0:T(8,128)(2,1)}, bf16[8,2,56,128]{3,2,1,0:T(8,128)(2,1)S(1)}, u32[]{:S(2)}) copy-start(bf16[8,2,56,128]{3,2,1,0:T(8,128)(2,1)S(1)} %all_to_all.17.refs_0_) | copy-start | bytes 688132
  128.3 6.1 %collective-permute-start.12 = (bf16[8,2,56,128]{3,2,1,0:T(8,128)(2,1)S(1)}, bf16[8,2,56,128]{3,2,1,0:T(8,128)(2,1)}, u32[]{:S(2)}, u32[]{:S(2)}) collective-permute-start(bf16[8,2,56,128]{3,2,1,0:T(8,128)(2,1)S(1)} %all_to_all.17.refs_0_), channel_id=1, source_target_pairs={{0,2},{1,3},{2,0},{3,1},{4,6},{5,7},{6,4},{7,5},{8,10},{9,11},{10,... | collective-permute-start | bytes 688136 | tf_op jit(solution)/shard_map/ppermute | solution.py:534
  129.8 6.7 %collective-permute-start.14 = (bf16[8,2,56,128]{3,2,1,0:T(8,128)(2,1)S(1)}, bf16[8,2,56,128]{3,2,1,0:T(8,128)(2,1)}, u32[]{:S(2)}, u32[]{:S(2)}) collective-permute-start(bf16[8,2,56,128]{3,2,1,0:T(8,128)(2,1)S(1)} %all_to_all.17.refs_0_), channel_id=1, source_target_pairs={{0,1},{1,0},{2,3},{3,2},{4,5},{5,4},{6,7},{7,6},{8,9},{9,8},{10,11... | collective-permute-start | bytes 688136 | tf_op jit(solution)/shard_map/ppermute | solution.py:534
  134.5 4.1 %collective-permute-start.13 = (bf16[8,2,56,128]{3,2,1,0:T(8,128)(2,1)}, bf16[8,2,56,128]{3,2,1,0:T(8,128)(2,1)}, u32[]{:S(2)}, u32[]{:S(2)}) collective-permute-start(bf16[8,2,56,128]{3,2,1,0:T(8,128)(2,1)} %collective-permute-done.12.refs_0_), channel_id=1, source_target_pairs={{0,1},{1,0},{2,3},{3,2},{4,5},{5,4},{6,7},{7,6},{8,9},{9,8},{10,11... | collective-permute-start | bytes 688136 | tf_op jit(solution)/shard_map/ppermute | solution.py:534

commit v2 on v1

--- a/solution.py
+++ b/solution.py
@@ -132,7 +132,7 @@
     keep = (lane > 0).astype(F32)
     low_lane = lane < (cols - main)
 
-    def one_coil(coil, carry):
+    def fold(coil):
         sums = {}
         for top in range(2):
             here = slice(top * half, top * half + half)
@@ -146,19 +146,22 @@
                 value = sums[0, part] + sums[1, part] if sign == 0 else sums[0, part] - sums[1, part]
                 high, low = split(value)
                 there = slice((2 * sign + part) * half, (2 * sign + part + 1) * half)
-                xcat[there, :main] = high[:, :main]
-                xcat[there, main : 2 * main] = low[:, :main]
-                xcat[there, 2 * main : 2 * main + LANES] = jnp.where(low_lane, high[:, main:], low[:, main:])
-                xcat[there, 2 * main + LANES :] = high[:, main:]
-
-        @pl.when(coil == 0)
-        def _():
-            moved[1].wait()
-
+                xcat[coil, there, :main] = high[:, :main]
+                xcat[coil, there, main : 2 * main] = low[:, :main]
+                xcat[coil, there, 2 * main : 2 * main + LANES] = jnp.where(low_lane, high[:, main:], low[:, main:])
+                xcat[coil, there, 2 * main + LANES :] = high[:, main:]
+
+    def columns(coil):
+        products = []
         for sign in range(2):
             lines = slice(2 * sign * half, (2 * sign + 2) * half)
-            spread = [xcat[lines, : 2 * main], xcat[lines, :main], xcat[lines, 2 * main :]]
-            both = dot(jnp.concatenate(spread, 1), tcol_ref[...])
+            spread = [xcat[coil, lines, : 2 * main], xcat[coil, lines, :main], xcat[coil, lines, 2 * main :]]
+            products.append(dot(jnp.concatenate(spread, 1), tcol_ref[...]))
+        return products
+
+    def mix_columns(coil, products):
+        for sign in range(2):
+            both = products[sign]
             re, im = both[:half], both[half:]
             for step in range(steps):
                 at = step * LANES
@@ -181,20 +184,24 @@
                 for part, value in enumerate((m_re, m_im)):
                     high, low = split(value)
                     there = slice((2 * step + part) * LANES, (2 * step + part + 1) * LANES)
-                    mid[sign, :half, there] = high
-                    mid[sign, half:, there] = low
-
-        @pl.when(coil == 0)
-        def _():
-            for copy in moved[2:6]:
-                copy.wait()
-
-        def one_step(step, carry):
-            there = pl.ds(pl.multiple_of(step * 2 * LANES, 2 * LANES), 2 * LANES)
-            here = pl.ds(pl.multiple_of(step * LANES, LANES), LANES)
-            even, odd = [
-                dot(trow_ref[sign], jnp.concatenate([mid[sign, :, there], mid[sign, :half, there]], 0)) for sign in range(2)
+                    mid[coil, sign, :half, there] = high
+                    mid[coil, sign, half:, there] = low
+
+
+    def rows_pass(coil):
+        def forward(step):
+            there = slice(step * 2 * LANES, (step + 1) * 2 * LANES)
+            return [
+                dot(trow_ref[sign], jnp.concatenate([mid[coil, sign, :, there], mid[coil, sign, :half, there]], 0)) for sign in range(2)
             ]
+
+        following = forward(0)
+        for step in range(steps):
+            there = slice(step * 2 * LANES, (step + 1) * 2 * LANES)
+            here = slice(step * LANES, (step + 1) * LANES)
+            even, odd = following
+            if step + 1 < steps:
+                following = forward(step + 1)
             sig, dif = sig_ref[:, here], dif_ref[:, here]
             c_re, c_im = even[:, :LANES], even[:, LANES:]
             s_re, s_im = odd[:, :LANES], odd[:, LANES:]
@@ -208,16 +215,15 @@
             for number, pair in enumerate(((p_re, p_im), (q_re, q_im))):
                 both = [split(value) for value in pair]
                 high, low = [jnp.concatenate([both[0][n], both[1][n]], 1) for n in range(2)]
-                back[number, :, there] = dot(tback_ref[number], jnp.concatenate([high, low, high], 0))
-            return carry
-
-        lax.fori_loop(0, steps, one_step, 0, unroll=True)
+                back[coil, number, :, there] = dot(tback_ref[number], jnp.concatenate([high, low, high], 0))
+
+    def unmix_columns(coil):
         for sign in range(2):
             for step in range(steps):
                 at = step * LANES
 
                 def piece(index, part):
-                    return back[sign, :, (2 * index + part) * LANES : (2 * index + part + 1) * LANES]
+                    return back[coil, sign, :, (2 * index + part) * LANES : (2 * index + part + 1) * LANES]
 
                 shift = main // LANES
                 if at < main:
@@ -239,15 +245,13 @@
                 for part, value in enumerate((w_re, w_im)):
                     high, low = split(value)
                     there = slice((2 * sign + part) * half, (2 * sign + part + 1) * half)
-                    last[there, at : at + LANES] = high
-                    last[there, spectral + at : spectral + at + LANES] = low
-
-        @pl.when(coil == 0)
-        def _():
-            moved[6].wait()
-            moved[7].wait()
-
-        final = dot(jnp.concatenate([last[...], last[:, :spectral]], 1), tlast_ref[...])
+                    last[coil, there, at : at + LANES] = high
+                    last[coil, there, spectral + at : spectral + at + LANES] = low
+
+    def last_columns(coil):
+        return dot(jnp.concatenate([last[coil], last[coil, :, :spectral]], 1), tlast_ref[...])
+
+    def add_residual(coil, final):
         plus_re, plus_im, minus_re, minus_im = [final[n * half : (n + 1) * half] for n in range(4)]
         for top in range(2):
             here = slice(top * half, top * half + half)
@@ -262,10 +266,26 @@
             s_im = sens_ref[coil, 1, here, :cols].astype(F32)
             acc[0, here] += s_re * n_re + s_im * n_im
             acc[1, here] += s_re * n_im - s_im * n_re
-        return carry
 
     acc[...] = jnp.zeros_like(acc)
-    lax.fori_loop(0, coils, one_coil, 0)
+    fold(0)
+    moved[1].wait()
+    products = columns(0)
+    for coil in range(coils):
+        if coil + 1 < coils:
+            fold(coil + 1)
+        mix_columns(coil, products)
+        if coil == 0:
+            for copy in moved[2:6]:
+                copy.wait()
+        rows_pass(coil)
+        if coil + 1 < coils:
+            products = columns(coil + 1)
+        unmix_columns(coil)
+        if coil == 0:
+            moved[6].wait()
+            moved[7].wait()
+        add_residual(coil, last_columns(coil))
     for part in range(2):
         above, below = acc[part, :half], acc[part, half:]
         high, low = split(below)
@@ -306,13 +326,13 @@
             pltpu.VMEM((size,) + packed, BF16),
             pltpu.VMEM((2, rows, cols), BF16),
             pltpu.VMEM((2, rows, wide), F32),
-            pltpu.VMEM((4 * half, tcol.shape[0] * 3 // 4), BF16),
-            pltpu.VMEM((2, 2 * half, 2 * spectral), BF16),
-            pltpu.VMEM((2, half, 2 * spectral), F32),
-            pltpu.VMEM((4 * half, 2 * spectral), BF16),
+            pltpu.VMEM((coils, 4 * half, tcol.shape[0] * 3 // 4), BF16),
+            pltpu.VMEM((coils, 2, 2 * half, 2 * spectral), BF16),
+            pltpu.VMEM((coils, 2, half, 2 * spectral), F32),
+            pltpu.VMEM((coils, 4 * half, 2 * spectral), BF16),
             pltpu.VMEM((2, rows, cols), F32),
         ],
-        compiler_params=pltpu.CompilerParams(vmem_limit_bytes=VMEM_BYTES),
+        compiler_params=pltpu.CompilerParams(vmem_limit_bytes=VMEM_BYTES - (1 << 20)),
         cost_estimate=pl.CostEstimate(flops=flops, bytes_accessed=8 * 1024 * 1024, transcendentals=0),
     )(me, *parts, sens, sig, dif, data, tcol, trow, tback, tlast, sig0, rev, *before)
 

time: 142 us -> 139 us (0.979)
  Pallas kernels: 54.2 us -> 51.9 us
    pallas_call x2, Pallas kernels: 34.6 us -> 32.3 us  [normal_call(): pl.pallas_call(functools.partial(normal_kernel, size, len(before), frame,...]
  transfers between devices with their start and end apart: 15 -> 15, of which waited for: 7 -> 7; matrix products, arithmetic and copies ran while one was open for 1% -> 1% of each run, Pallas kernels for 9% -> 10%
where the time goes in v2:
time: 139 us; the launch traced here: 138 us
  Pallas kernels  51.9 us (37%)
  blocking collectives  41.8 us (30%)
  waiting for transfers between devices  25.8 us (19%)
  starting transfers between devices  15.5 us (11%)
  other arithmetic  2.46 us (2%)
    all_to_all x3, blocking collectives, swap(): lax.all_to_all(value, 'frame', split_axis=0, concat_axis=0, tiled=True)  41.8 us
    pallas_call x2, Pallas kernels, normal_call(): pl.pallas_call(functools.partial(normal_kernel, size, len(before), frame,...  32.3 us
    ppermute x15, waiting for transfers between devices, exchange(): return lax.ppermute(value, axis, [(i, i ^ distance) for i in range(size)])  25.8 us
    ppermute x15, starting transfers between devices, exchange(): return lax.ppermute(value, axis, [(i, i ^ distance) for i in range(size)])  15.5 us
    pallas_call x1, Pallas kernels, prepare_call(): pl.pallas_call(prepare_kernel, grid=(frames,), out_shape=(jax.ShapeDtypeS...  7.06 us
    pallas_call x2, Pallas kernels, place_call(): pl.pallas_call(functools.partial(place_kernel, numbers, len(before)), out...  4.22 us
  transfers between devices with their start and end apart: 15, of which 7 were waited for; matrix products, arithmetic and copies ran while one was open for 1% of the time, Pallas kernels for 10%

profile of v2, /device:TPU:0, one launch (start us, length us, event | category | flops | bytes accessed | tf_op | source)
XLA Modules:
  0.0 138.4 jit_solution(14120969092384864944)
XLA Ops:
  0.6 3.1 %collective-permute-start = (f32[1,2,8]{2,1,0:T(2,128)}, f32[1,2,8]{2,1,0:T(2,128)S(1)}, u32[]{:S(2)}, u32[]{:S(2)}) collective-permute-start(f32[1,2,8]{2,1,0:T(2,128)} %bitcast.10), channel_id=1, source_target_pairs={{0,4},{4,0},{8,12},{12,8},{16,20},{20,16},{24,28},{28,24},{1,5},{5... | collective-permute-start | bytes 200 | tf_op jit(solution)/shard_map/ppermute | solution.py:554
  3.7 1.8 %collective-permute-done = f32[1,2,8]{2,1,0:T(2,128)S(1)} collective-permute-done((f32[1,2,8]{2,1,0:T(2,128)}, f32[1,2,8]{2,1,0:T(2,128)S(1)}, u32[]{:S(2)}, u32[]{:S(2)}) %collective-permute-start) | collective-permute-done | bytes 96 | tf_op jit(solution)/shard_map/ppermute | solution.py:554
  5.5 0.8 maximum_select_fusion.2
  6.2 2.1 %collective-permute-start.1 = (f32[2,2,8]{2,1,0:T(2,128)S(1)}, f32[2,2,8]{2,1,0:T(2,128)S(1)}, u32[]{:S(2)}, u32[]{:S(2)}) collective-permute-start(f32[2,2,8]{2,1,0:T(2,128)S(1)} %maximum_select_fusion.2), channel_id=1, source_target_pairs={{0,8},{4,12},{8,0},{12,4},{16,24},{20,28},{24,16},{28,20},{1,9},{5... | collective-permute-start | bytes 392 | tf_op jit(solution)/shard_map/ppermute | solution.py:554
  8.3 1.6 %collective-permute-done.1 = f32[2,2,8]{2,1,0:T(2,128)S(1)} collective-permute-done((f32[2,2,8]{2,1,0:T(2,128)S(1)}, f32[2,2,8]{2,1,0:T(2,128)S(1)}, u32[]{:S(2)}, u32[]{:S(2)}) %collective-permute-start.1) | collective-permute-done | bytes 160 | tf_op jit(solution)/shard_map/ppermute | solution.py:554
  9.9 3.0 %collective-permute-start.2 = (f32[4,2,8]{2,1,0:T(2,128)S(1)}, f32[4,2,8]{2,1,0:T(2,128)S(1)}, u32[]{:S(2)}, u32[]{:S(2)}) collective-permute-start(f32[4,2,8]{2,1,0:T(2,128)S(1)} %maximum_select_fusion.1), channel_id=1, source_target_pairs={{0,16},{4,20},{8,24},{12,28},{16,0},{20,4},{24,8},{28,12},{1,17},{... | collective-permute-start | bytes 776 | tf_op jit(solution)/shard_map/ppermute | solution.py:554
  12.9 2.0 %shard_map.149.factor_ref = f32[8,56,128]{2,1,0:T(8,128)} custom-call(f32[8,2,40,80]{3,2,1,0:T(8,128)} %bitcast.8), custom_call_target="tpu_custom_call" | custom-call | tf_op jit(solution)/shard_map/pallas_call | solution.py:395
  14.9 0.6 maximum_select_fusion.temporal_ref
  15.5 1.9 %shard_map.150.after_ref = bf16[8,2,56,128]{3,2,1,0:T(8,128)(2,1)} custom-call(f32[8,2,8]{2,1,0:T(2,128)} %maximum_select_fusion.temporal_ref, f32[8,56,128]{2,1,0:T(8,128)} %shard_map.149.factor_ref), custom_call_target="tpu_custom_call" | custom-call | tf_op jit(solution)/shard_map/pallas_call | solution.py:439
  17.4 13.8 %all_to_all.15.refs_0_ = bf16[8,2,56,128]{3,2,1,0:T(8,128)(2,1)} all-to-all(bf16[8,2,56,128]{3,2,1,0:T(8,128)(2,1)} %shard_map.150.after_ref), channel_id=1, replica_groups=mesh['frame'=8,'coil'=4] {'frame'}, dimensions={0} | all-to-all | bytes 458752 | tf_op jit(solution)/shard_map/all_to_all | solution.py:601
  31.3 1.5 %collective-permute-start.4 = (bf16[8,2,56,128]{3,2,1,0:T(8,128)(2,1)}, bf16[8,2,56,128]{3,2,1,0:T(8,128)(2,1)}, u32[]{:S(2)}, u32[]{:S(2)}) collective-permute-start(bf16[8,2,56,128]{3,2,1,0:T(8,128)(2,1)} %all_to_all.15.refs_0_), channel_id=1, source_target_pairs={{0,2},{1,3},{2,0},{3,1},{4,6},{5,7},{6,4},{7,5},{8,10},{9,11},{10,... | collective-permute-start | bytes 688136 | tf_op jit(solution)/shard_map/ppermute | solution.py:554
  32.8 4.8 %collective-permute-done.4.refs_2_ = bf16[8,2,56,128]{3,2,1,0:T(8,128)(2,1)} collective-permute-done((bf16[8,2,56,128]{3,2,1,0:T(8,128)(2,1)}, bf16[8,2,56,128]{3,2,1,0:T(8,128)(2,1)}, u32[]{:S(2)}, u32[]{:S(2)}) %collective-permute-start.4) | collective-permute-done | bytes 229408 | tf_op jit(solution)/shard_map/ppermute | solution.py:554
  37.6 7.1 %shard_map.151 = (f32[2,320,640]{2,1,0:T(8,128)}, f32[2,320,640]{2,1,0:T(8,128)}, f32[2,8,640]{2,1,0:T(8,128)}, bf16[2,2,320,384]{3,2,1,0:T(8,128)(2,1)}) custom-call(s32[2,640,640]{2,1,0:T(8,128)} %index_ref.1, f32[2,8]{1,0:T(2,128)} %level_ref.1, bf16[2,2,320,320]{3,2,1,0:T(8,128)(2,1)} %sens_ref.1, bf16[320,320]{1,0:T(8,128)(2,1)} %constant.81.clone.row_ref, ...), custom_call_target="tpu_custom_call" | custom-call | flops 1572864000 | bytes 16777216 | tf_op jit(solution)/shard_map/pallas_call | solution.py:507
  44.7 16.0 %shard_map.152 = (f32[8,56,128]{2,1,0:T(8,128)}, f32[8,56,128]{2,1,0:T(8,128)}, f32[8,56,128]{2,1,0:T(8,128)}, f32[8,56,128]{2,1,0:T(8,128)}) custom-call(s32[1]{0:T(128)} %bitcast.2.me_ref, bf16[8,2,56,128]{3,2,1,0:T(8,128)(2,1)} %all_to_all.15.refs_0_, bf16[8,2,56,128]{3,2,1,0:T(8,128)(2,1)} %collective-permute-done.3.refs_1_, ...), custom_call_target="tpu_custom_call" | custom-call | flops 6291456000 | bytes 8388608 | tf_op jit(solution)/shard_map/pallas_call | solution.py:318
  60.7 16.3 %shard_map.153 = (f32[8,56,128]{2,1,0:T(8,128)}, f32[8,56,128]{2,1,0:T(8,128)}, f32[8,56,128]{2,1,0:T(8,128)}, f32[8,56,128]{2,1,0:T(8,128)}) custom-call(s32[1]{0:T(128)} %bitcast.2.me_ref, bf16[8,2,56,128]{3,2,1,0:T(8,128)(2,1)} %all_to_all.15.refs_0_, bf16[8,2,56,128]{3,2,1,0:T(8,128)(2,1)} %collective-permute-done.3.refs_1_, ...), custom_call_target="tpu_custom_call" | custom-call | flops 6291456000 | bytes 8388608 | tf_op jit(solution)/shard_map/pallas_call | solution.py:318
  77.0 0.6 collective-permute-start.10
  77.6 1.5 %collective-permute-start.7 = (f32[8,56,128]{2,1,0:T(8,128)S(1)}, f32[8,56,128]{2,1,0:T(8,128)S(1)}, u32[]{:S(2)}, u32[]{:S(2)}) collective-permute-start(f32[8,56,128]{2,1,0:T(8,128)S(1)} %copy-done.4), channel_id=1, source_target_pairs={{0,2},{1,3},{2,0},{3,1},{4,6},{5,7},{6,4},{7,5},{8,10},{9,11},{10,... | collective-permute-start | bytes 688136 | tf_op jit(solution)/shard_map/ppermute | solution.py:554
  79.1 0.3 collective-permute-start.8
  79.4 0.4 collective-permute-start.9
  79.8 1.0 add.38
  80.8 1.6 %collective-permute-start.11 = (f32[8,56,128]{2,1,0:T(8,128)S(1)}, f32[8,56,128]{2,1,0:T(8,128)S(1)}, u32[]{:S(2)}, u32[]{:S(2)}) collective-permute-start(f32[8,56,128]{2,1,0:T(8,128)S(1)} %add.38), channel_id=1, source_target_pairs={{0,2},{1,3},{2,0},{3,1},{4,6},{5,7},{6,4},{7,5},{8,10},{9,11},{10,... | collective-permute-start | bytes 688136 | tf_op jit(solution)/shard_map/ppermute | solution.py:554
  82.3 3.8 %collective-permute-done.7 = f32[8,56,128]{2,1,0:T(8,128)S(1)} collective-permute-done((f32[8,56,128]{2,1,0:T(8,128)S(1)}, f32[8,56,128]{2,1,0:T(8,128)S(1)}, u32[]{:S(2)}, u32[]{:S(2)}) %collective-permute-start.7) | collective-permute-done | bytes 229408 | tf_op jit(solution)/shard_map/ppermute | solution.py:554
  86.1 3.9 %collective-permute-done.8 = f32[8,56,128]{2,1,0:T(8,128)S(1)} collective-permute-done((f32[8,56,128]{2,1,0:T(8,128)S(1)}, f32[8,56,128]{2,1,0:T(8,128)S(1)}, u32[]{:S(2)}, u32[]{:S(2)}) %collective-permute-start.8) | collective-permute-done | bytes 229408 | tf_op jit(solution)/shard_map/ppermute | solution.py:554
  90.1 5.3 %collective-permute-done.11 = f32[8,56,128]{2,1,0:T(8,128)S(1)} collective-permute-done((f32[8,56,128]{2,1,0:T(8,128)S(1)}, f32[8,56,128]{2,1,0:T(8,128)S(1)}, u32[]{:S(2)}, u32[]{:S(2)}) %collective-permute-start.11) | collective-permute-done | bytes 229408 | tf_op jit(solution)/shard_map/ppermute | solution.py:554
  95.5 16.3 %all_to_all.16.residual_ref = f32[8,2,56,128]{3,2,1,0:T(8,128)} all-to-all(f32[8,2,56,128]{3,2,1,0:T(8,128)S(1)} %pad_maximum_fusion), channel_id=1, replica_groups=mesh['frame'=8,'coil'=4] {'frame'}, dimensions={0} | all-to-all | bytes 917504 | tf_op jit(solution)/shard_map/all_to_all | solution.py:601
  111.8 2.4 %shard_map.154 = (f32[8,56,128]{2,1,0:T(8,128)}, bf16[8,2,56,128]{3,2,1,0:T(8,128)(2,1)}) custom-call(f32[8,2,8]{2,1,0:T(2,128)} %maximum_select_fusion.temporal_ref, f32[8,56,128]{2,1,0:T(8,128)} %shard_map.149.factor_ref, f32[8,2,56,128]{3,2,1,0:T(8,128)} %all_to_all.16.residual_ref), custom_call_target="tpu_custom_call" | custom-call | tf_op jit(solution)/shard_map/pallas_call | solution.py:449
  114.1 11.7 %all_to_all.17.refs_0_ = bf16[8,2,56,128]{3,2,1,0:T(8,128)(2,1)S(1)} all-to-all(bf16[8,2,56,128]{3,2,1,0:T(8,128)(2,1)} %get-tuple-element.29), channel_id=1, replica_groups=mesh['frame'=8,'coil'=4] {'frame'}, dimensions={0} | all-to-all | bytes 458752 | tf_op jit(solution)/shard_map/all_to_all | solution.py:601
  125.9 1.5 %collective-permute-start.12 = (bf16[8,2,56,128]{3,2,1,0:T(8,128)(2,1)S(1)}, bf16[8,2,56,128]{3,2,1,0:T(8,128)(2,1)}, u32[]{:S(2)}, u32[]{:S(2)}) collective-permute-start(bf16[8,2,56,128]{3,2,1,0:T(8,128)(2,1)S(1)} %all_to_all.17.refs_0_), channel_id=1, source_target_pairs={{0,2},{1,3},{2,0},{3,1},{4,6},{5,7},{6,4},{7,5},{8,10},{9,11},{10,... | collective-permute-start | bytes 688136 | tf_op jit(solution)/shard_map/ppermute | solution.py:554
  127.4 4.6 %collective-permute-done.12.refs_0_ = bf16[8,2,56,128]{3,2,1,0:T(8,128)(2,1)} collective-permute-done((bf16[8,2,56,128]{3,2,1,0:T(8,128)(2,1)S(1)}, bf16[8,2,56,128]{3,2,1,0:T(8,128)(2,1)}, u32[]{:S(2)}, u32[]{:S(2)}) %collective-permute-start.12) | collective-permute-done | bytes 229408 | tf_op jit(solution)/shard_map/ppermute | solution.py:554
  132.0 2.0 %shard_map.155 = f32[8,2,40,80]{3,2,1,0:T(8,128)} custom-call(f32[8,56,128]{2,1,0:T(8,128)} %get-tuple-element.28.packed_ref), custom_call_target="tpu_custom_call" | custom-call | tf_op jit(solution)/shard_map/pallas_call | solution.py:407
  134.0 2.1 %shard_map.156.refs_2_ = bf16[2,2,320,320]{3,2,1,0:T(8,128)(2,1)} custom-call(s32[1]{0:T(128)} %bitcast.2.me_ref, bf16[8,2,56,128]{3,2,1,0:T(8,128)(2,1)} %copy-done, bf16[8,2,56,128]{3,2,1,0:T(8,128)(2,1)} %collective-permute-done.14.refs_1_), custom_call_target="tpu_custom_call" | custom-call | flops 1048576 | bytes 4194304 | tf_op jit(solution)/shard_map/pallas_call | solution.py:369
  136.1 2.1 %shard_map.157 = bf16[2,2,320,320]{3,2,1,0:T(8,128)(2,1)} custom-call(s32[1]{0:T(128)} %bitcast.2.me_ref, bf16[8,2,56,128]{3,2,1,0:T(8,128)(2,1)} %collective-permute-done.12.refs_0_, bf16[8,2,56,128]{3,2,1,0:T(8,128)(2,1)} %collective-permute-done.13.refs_1_, bf16[2,2,320,320]{3,2,1,0:T(8,128)(2,1)} %shard_map.156.refs_2_), custom_call_target="tpu_custom_call", output_to_operand_aliasing={{}: (3, {})} | custom-call | flops 1048576 | bytes 4194304 | tf_op jit(solution)/shard_map/pallas_call | solution.py:369
  (29 shorter events, 0.3 us)
Async XLA Ops:
  0.6 4.8 %collective-permute-start = (f32[1,2,8]{2,1,0:T(2,128)}, f32[1,2,8]{2,1,0:T(2,128)S(1)}, u32[]{:S(2)}, u32[]{:S(2)}) collective-permute-start(f32[1,2,8]{2,1,0:T(2,128)} %bitcast.10), channel_id=1, source_target_pairs={{0,4},{4,0},{8,12},{12,8},{16,20},{20,16},{24,28},{28,24},{1,5},{5... | collective-permute-start | bytes 200 | tf_op jit(solution)/shard_map/ppermute | solution.py:554
  6.2 3.6 %collective-permute-start.1 = (f32[2,2,8]{2,1,0:T(2,128)S(1)}, f32[2,2,8]{2,1,0:T(2,128)S(1)}, u32[]{:S(2)}, u32[]{:S(2)}) collective-permute-start(f32[2,2,8]{2,1,0:T(2,128)S(1)} %maximum_select_fusion.2), channel_id=1, source_target_pairs={{0,8},{4,12},{8,0},{12,4},{16,24},{20,28},{24,16},{28,20},{1,9},{5... | collective-permute-start | bytes 392 | tf_op jit(solution)/shard_map/ppermute | solution.py:554
  9.9 5.1 %collective-permute-start.2 = (f32[4,2,8]{2,1,0:T(2,128)S(1)}, f32[4,2,8]{2,1,0:T(2,128)S(1)}, u32[]{:S(2)}, u32[]{:S(2)}) collective-permute-start(f32[4,2,8]{2,1,0:T(2,128)S(1)} %maximum_select_fusion.1), channel_id=1, source_target_pairs={{0,16},{4,20},{8,24},{12,28},{16,0},{20,4},{24,8},{28,12},{1,17},{... | collective-permute-start | bytes 776 | tf_op jit(solution)/shard_map/ppermute | solution.py:554
  31.3 6.3 %collective-permute-start.4 = (bf16[8,2,56,128]{3,2,1,0:T(8,128)(2,1)}, bf16[8,2,56,128]{3,2,1,0:T(8,128)(2,1)}, u32[]{:S(2)}, u32[]{:S(2)}) collective-permute-start(bf16[8,2,56,128]{3,2,1,0:T(8,128)(2,1)} %all_to_all.15.refs_0_), channel_id=1, source_target_pairs={{0,2},{1,3},{2,0},{3,1},{4,6},{5,7},{6,4},{7,5},{8,10},{9,11},{10,... | collective-permute-start | bytes 688136 | tf_op jit(solution)/shard_map/ppermute | solution.py:554
  32.7 11.9 %collective-permute-start.3 = (bf16[8,2,56,128]{3,2,1,0:T(8,128)(2,1)}, bf16[8,2,56,128]{3,2,1,0:T(8,128)(2,1)}, u32[]{:S(2)}, u32[]{:S(2)}) collective-permute-start(bf16[8,2,56,128]{3,2,1,0:T(8,128)(2,1)} %all_to_all.15.refs_0_), channel_id=1, source_target_pairs={{0,1},{1,0},{2,3},{3,2},{4,5},{5,4},{6,7},{7,6},{8,9},{9,8},{10,11... | collective-permute-start | bytes 688136 | tf_op jit(solution)/shard_map/ppermute | solution.py:554
  37.6 7.1 %collective-permute-start.5 = (bf16[8,2,56,128]{3,2,1,0:T(8,128)(2,1)}, bf16[8,2,56,128]{3,2,1,0:T(8,128)(2,1)}, u32[]{:S(2)}, u32[]{:S(2)}) collective-permute-start(bf16[8,2,56,128]{3,2,1,0:T(8,128)(2,1)} %collective-permute-done.4.refs_2_), channel_id=1, source_target_pairs={{0,1},{1,0},{2,3},{3,2},{4,5},{5,4},{6,7},{7,6},{8,9},{9,8},{10,11... | collective-permute-start | bytes 688136 | tf_op jit(solution)/shard_map/ppermute | solution.py:554
  60.6 16.9 %copy-start.5 = (f32[8,56,128]{2,1,0:T(8,128)S(1)}, f32[8,56,128]{2,1,0:T(8,128)}, u32[]{:S(2)}) copy-start(f32[8,56,128]{2,1,0:T(8,128)} %get-tuple-element.21) | copy-start | bytes 688132
  60.7 17.0 %copy-start.4 = (f32[8,56,128]{2,1,0:T(8,128)S(1)}, f32[8,56,128]{2,1,0:T(8,128)}, u32[]{:S(2)}) copy-start(f32[8,56,128]{2,1,0:T(8,128)} %get-tuple-element.22) | copy-start | bytes 688132
  60.7 18.5 %copy-start.3 = (f32[8,56,128]{2,1,0:T(8,128)S(1)}, f32[8,56,128]{2,1,0:T(8,128)}, u32[]{:S(2)}) copy-start(f32[8,56,128]{2,1,0:T(8,128)} %get-tuple-element.23) | copy-start | bytes 688132
  60.7 29.4 %copy-start.2 = (f32[8,56,128]{2,1,0:T(8,128)S(1)}, f32[8,56,128]{2,1,0:T(8,128)}, u32[]{:S(2)}) copy-start(f32[8,56,128]{2,1,0:T(8,128)} %get-tuple-element.20.refs_14_) | copy-start | bytes 688132
  77.0 18.4 %copy-start.1 = (f32[8,56,128]{2,1,0:T(8,128)S(1)}, f32[8,56,128]{2,1,0:T(8,128)}, u32[]{:S(2)}) copy-start(f32[8,56,128]{2,1,0:T(8,128)} %get-tuple-element.24) | copy-start | bytes 688132
  77.0 2.8 %collective-permute-start.10 = (f32[8,56,128]{2,1,0:T(8,128)}, f32[8,56,128]{2,1,0:T(8,128)S(1)}, u32[]{:S(2)}, u32[]{:S(2)}) collective-permute-start(f32[8,56,128]{2,1,0:T(8,128)} %get-tuple-element.27), channel_id=1, source_target_pairs={{0,1},{1,0},{2,3},{3,2},{4,5},{5,4},{6,7},{7,6},{8,9},{9,8},{10,11... | collective-permute-start | bytes 688136 | tf_op jit(solution)/shard_map/ppermute | solution.py:554
  77.5 4.8 %collective-permute-start.6 = (f32[8,56,128]{2,1,0:T(8,128)S(1)}, f32[8,56,128]{2,1,0:T(8,128)S(1)}, u32[]{:S(2)}, u32[]{:S(2)}) collective-permute-start(f32[8,56,128]{2,1,0:T(8,128)S(1)} %copy-done.5), channel_id=1, source_target_pairs={{0,1},{1,0},{2,3},{3,2},{4,5},{5,4},{6,7},{7,6},{8,9},{9,8},{10,11... | collective-permute-start | bytes 688136 | tf_op jit(solution)/shard_map/ppermute | solution.py:554
  77.6 8.5 %collective-permute-start.7 = (f32[8,56,128]{2,1,0:T(8,128)S(1)}, f32[8,56,128]{2,1,0:T(8,128)S(1)}, u32[]{:S(2)}, u32[]{:S(2)}) collective-permute-start(f32[8,56,128]{2,1,0:T(8,128)S(1)} %copy-done.4), channel_id=1, source_target_pairs={{0,2},{1,3},{2,0},{3,1},{4,6},{5,7},{6,4},{7,5},{8,10},{9,11},{10,... | collective-permute-start | bytes 688136 | tf_op jit(solution)/shard_map/ppermute | solution.py:554
  79.1 10.9 %collective-permute-start.8 = (f32[8,56,128]{2,1,0:T(8,128)S(1)}, f32[8,56,128]{2,1,0:T(8,128)S(1)}, u32[]{:S(2)}, u32[]{:S(2)}) collective-permute-start(f32[8,56,128]{2,1,0:T(8,128)S(1)} %copy-done.3), channel_id=1, source_target_pairs={{0,3},{1,2},{2,1},{3,0},{4,7},{5,6},{6,5},{7,4},{8,11},{9,10},{10,... | collective-permute-start | bytes 688136 | tf_op jit(solution)/shard_map/ppermute | solution.py:554
  79.4 10.7 %collective-permute-start.9 = (f32[8,56,128]{2,1,0:T(8,128)}, f32[8,56,128]{2,1,0:T(8,128)S(1)}, u32[]{:S(2)}, u32[]{:S(2)}) collective-permute-start(f32[8,56,128]{2,1,0:T(8,128)} %get-tuple-element.25), channel_id=1, source_target_pairs={{0,1},{1,0},{2,3},{3,2},{4,5},{5,4},{6,7},{7,6},{8,9},{9,8},{10,11... | collective-permute-start | bytes 688136 | tf_op jit(solution)/shard_map/ppermute | solution.py:554
  80.8 14.6 %collective-permute-start.11 = (f32[8,56,128]{2,1,0:T(8,128)S(1)}, f32[8,56,128]{2,1,0:T(8,128)S(1)}, u32[]{:S(2)}, u32[]{:S(2)}) collective-permute-start(f32[8,56,128]{2,1,0:T(8,128)S(1)} %add.38), channel_id=1, source_target_pairs={{0,2},{1,3},{2,0},{3,1},{4,6},{5,7},{6,4},{7,5},{8,10},{9,11},{10,... | collective-permute-start | bytes 688136 | tf_op jit(solution)/shard_map/ppermute | solution.py:554
  125.9 1.5 %copy-start = (bf16[8,2,56,128]{3,2,1,0:T(8,128)(2,1)}, bf16[8,2,56,128]{3,2,1,0:T(8,128)(2,1)S(1)}, u32[]{:S(2)}) copy-start(bf16[8,2,56,128]{3,2,1,0:T(8,128)(2,1)S(1)} %all_to_all.17.refs_0_) | copy-start | bytes 688132
  125.9 6.1 %collective-permute-start.12 = (bf16[8,2,56,128]{3,2,1,0:T(8,128)(2,1)S(1)}, bf16[8,2,56,128]{3,2,1,0:T(8,128)(2,1)}, u32[]{:S(2)}, u32[]{:S(2)}) collective-permute-start(bf16[8,2,56,128]{3,2,1,0:T(8,128)(2,1)S(1)} %all_to_all.17.refs_0_), channel_id=1, source_target_pairs={{0,2},{1,3},{2,0},{3,1},{4,6},{5,7},{6,4},{7,5},{8,10},{9,11},{10,... | collective-permute-start | bytes 688136 | tf_op jit(solution)/shard_map/ppermute | solution.py:554
  127.4 6.7 %collective-permute-start.14 = (bf16[8,2,56,128]{3,2,1,0:T(8,128)(2,1)S(1)}, bf16[8,2,56,128]{3,2,1,0:T(8,128)(2,1)}, u32[]{:S(2)}, u32[]{:S(2)}) collective-permute-start(bf16[8,2,56,128]{3,2,1,0:T(8,128)(2,1)S(1)} %all_to_all.17.refs_0_), channel_id=1, source_target_pairs={{0,1},{1,0},{2,3},{3,2},{4,5},{5,4},{6,7},{7,6},{8,9},{9,8},{10,11... | collective-permute-start | bytes 688136 | tf_op jit(solution)/shard_map/ppermute | solution.py:554
  132.0 4.1 %collective-permute-start.13 = (bf16[8,2,56,128]{3,2,1,0:T(8,128)(2,1)}, bf16[8,2,56,128]{3,2,1,0:T(8,128)(2,1)}, u32[]{:S(2)}, u32[]{:S(2)}) collective-permute-start(bf16[8,2,56,128]{3,2,1,0:T(8,128)(2,1)} %collective-permute-done.12.refs_0_), channel_id=1, source_target_pairs={{0,1},{1,0},{2,3},{3,2},{4,5},{5,4},{6,7},{7,6},{8,9},{9,8},{10,11... | collective-permute-start | bytes 688136 | tf_op jit(solution)/shard_map/ppermute | solution.py:554

commit v3 on v2

--- a/solution.py
+++ b/solution.py
@@ -332,30 +332,26 @@
             pltpu.VMEM((coils, 4 * half, 2 * spectral), BF16),
             pltpu.VMEM((2, rows, cols), F32),
         ],
-        compiler_params=pltpu.CompilerParams(vmem_limit_bytes=VMEM_BYTES - (1 << 20)),
+        compiler_params=pltpu.CompilerParams(vmem_limit_bytes=VMEM_BYTES - (9 << 17)),
         cost_estimate=pl.CostEstimate(flops=flops, bytes_accessed=8 * 1024 * 1024, transcendentals=0),
     )(me, *parts, sens, sig, dif, data, tcol, trow, tback, tlast, sig0, rev, *before)
 
 
 def place_kernel(numbers, extra, me_ref, *refs):
     total = len(numbers)
-    parts_hbm, out_hbm = refs[:total], refs[total + extra]
-    parts, blocks, sems = refs[total + extra + 1 :]
-    _, devices, frames, _, _ = parts.shape
+    parts_in, out_hbm = refs[:total], refs[total + extra]
+    blocks, sems = refs[total + extra + 1 :]
+    devices, frames = parts_in[0].shape[:2]
     count = blocks.shape[3]
     width = blocks.shape[4] // devices
-    arrived = [pltpu.make_async_copy(parts_hbm[n], parts.at[n], sems.at[n]) for n in range(total)]
-    for copy in arrived:
-        copy.start()
     leaving = []
     for n, number in enumerate(numbers):
-        arrived[n].wait()
         for frame in range(frames):
-            block = unpack([parts[n, device, frame].astype(F32) for device in range(devices)], 2 * count, width)
+            block = unpack([parts_in[n][device, frame].astype(F32) for device in range(devices)], 2 * count, width)
             for part in range(2):
                 blocks[n, frame, part] = block[part * count : (part + 1) * count].astype(BF16)
         there = pl.ds(pl.multiple_of((me_ref[0] ^ number) * count, count), count)
-        leaving.append(pltpu.make_async_copy(blocks.at[n], out_hbm.at[:, :, there], sems.at[total + n]))
+        leaving.append(pltpu.make_async_copy(blocks.at[n], out_hbm.at[:, :, there], sems.at[n]))
         leaving[-1].start()
     for copy in leaving:
         copy.wait()
@@ -365,19 +361,19 @@
     numbers = sorted(parts)
     devices, frames = parts[numbers[0]].shape[:2]
     away = pl.BlockSpec(memory_space=pl.ANY)
+    held = pl.BlockSpec(memory_space=pltpu.VMEM)
     total = len(numbers)
     return pl.pallas_call(
         functools.partial(place_kernel, numbers, len(before)),
         out_shape=jax.ShapeDtypeStruct((frames, 2, count * size, width * devices), BF16),
-        in_specs=[pl.BlockSpec(memory_space=pltpu.SMEM)] + [away] * (total + len(before)),
+        in_specs=[pl.BlockSpec(memory_space=pltpu.SMEM)] + [held] * total + [away] * len(before),
         out_specs=away,
         input_output_aliases={1 + total: 0} if before else {},
         scratch_shapes=[
-            pltpu.VMEM((total,) + parts[numbers[0]].shape, BF16),
             pltpu.VMEM((total, frames, 2, count, width * devices), BF16),
-            pltpu.SemaphoreType.DMA((2 * total,)),
+            pltpu.SemaphoreType.DMA((total,)),
         ],
-        compiler_params=pltpu.CompilerParams(vmem_limit_bytes=VMEM_BYTES),
+        compiler_params=pltpu.CompilerParams(vmem_limit_bytes=VMEM_BYTES // 4),
         cost_estimate=pl.CostEstimate(flops=1 << 20, bytes_accessed=4 * 1024 * 1024, transcendentals=0),
     )(me, *[parts[number] for number in numbers], *before)
 

time: 139 us -> 137 us (0.986)
  Pallas kernels: 51.9 us -> 49.8 us
    pallas_call x2, Pallas kernels: 4.22 us -> 2.16 us  [place_call(): pl.pallas_call(functools.partial(place_kernel, numbers, len(before)), out...]
  transfers between devices with their start and end apart: 15 -> 15, of which waited for: 7 -> 7; matrix products, arithmetic and copies ran while one was open for 1% -> 1% of each run, Pallas kernels for 10% -> 9%
where the time goes in v3:
time: 137 us; the launch traced here: 136 us
  Pallas kernels  49.8 us (36%)
  blocking collectives  41.8 us (31%)
  waiting for transfers between devices  25.7 us (19%)
  starting transfers between devices  15.5 us (11%)
  other arithmetic  2.46 us (2%)
    all_to_all x3, blocking collectives, swap(): lax.all_to_all(value, 'frame', split_axis=0, concat_axis=0, tiled=True)  41.8 us
    pallas_call x2, Pallas kernels, normal_call(): pl.pallas_call(functools.partial(normal_kernel, size, len(before), frame,...  32.2 us
    ppermute x15, waiting for transfers between devices, exchange(): return lax.ppermute(value, axis, [(i, i ^ distance) for i in range(size)])  25.7 us
    ppermute x15, starting transfers between devices, exchange(): return lax.ppermute(value, axis, [(i, i ^ distance) for i in range(size)])  15.5 us
    pallas_call x1, Pallas kernels, prepare_call(): pl.pallas_call(prepare_kernel, grid=(frames,), out_shape=(jax.ShapeDtypeS...  7.06 us
  transfers between devices with their start and end apart: 15, of which 7 were waited for; matrix products, arithmetic and copies ran while one was open for 1% of the time, Pallas kernels for 9%

profile of v3, /device:TPU:0, one launch (start us, length us, event | category | flops | bytes accessed | tf_op | source)
XLA Modules:
  0.0 136.3 jit_solution(8183557544960218135)
XLA Ops:
  0.6 3.1 %collective-permute-start = (f32[1,2,8]{2,1,0:T(2,128)}, f32[1,2,8]{2,1,0:T(2,128)S(1)}, u32[]{:S(2)}, u32[]{:S(2)}) collective-permute-start(f32[1,2,8]{2,1,0:T(2,128)} %bitcast.10), channel_id=1, source_target_pairs={{0,4},{4,0},{8,12},{12,8},{16,20},{20,16},{24,28},{28,24},{1,5},{5... | collective-permute-start | bytes 200 | tf_op jit(solution)/shard_map/ppermute | solution.py:550
  3.7 1.8 %collective-permute-done = f32[1,2,8]{2,1,0:T(2,128)S(1)} collective-permute-done((f32[1,2,8]{2,1,0:T(2,128)}, f32[1,2,8]{2,1,0:T(2,128)S(1)}, u32[]{:S(2)}, u32[]{:S(2)}) %collective-permute-start) | collective-permute-done | bytes 96 | tf_op jit(solution)/shard_map/ppermute | solution.py:550
  5.5 0.8 maximum_select_fusion.2
  6.2 2.1 %collective-permute-start.1 = (f32[2,2,8]{2,1,0:T(2,128)S(1)}, f32[2,2,8]{2,1,0:T(2,128)S(1)}, u32[]{:S(2)}, u32[]{:S(2)}) collective-permute-start(f32[2,2,8]{2,1,0:T(2,128)S(1)} %maximum_select_fusion.2), channel_id=1, source_target_pairs={{0,8},{4,12},{8,0},{12,4},{16,24},{20,28},{24,16},{28,20},{1,9},{5... | collective-permute-start | bytes 392 | tf_op jit(solution)/shard_map/ppermute | solution.py:550
  8.3 1.6 %collective-permute-done.1 = f32[2,2,8]{2,1,0:T(2,128)S(1)} collective-permute-done((f32[2,2,8]{2,1,0:T(2,128)S(1)}, f32[2,2,8]{2,1,0:T(2,128)S(1)}, u32[]{:S(2)}, u32[]{:S(2)}) %collective-permute-start.1) | collective-permute-done | bytes 160 | tf_op jit(solution)/shard_map/ppermute | solution.py:550
  9.9 3.0 %collective-permute-start.2 = (f32[4,2,8]{2,1,0:T(2,128)S(1)}, f32[4,2,8]{2,1,0:T(2,128)S(1)}, u32[]{:S(2)}, u32[]{:S(2)}) collective-permute-start(f32[4,2,8]{2,1,0:T(2,128)S(1)} %maximum_select_fusion.1), channel_id=1, source_target_pairs={{0,16},{4,20},{8,24},{12,28},{16,0},{20,4},{24,8},{28,12},{1,17},{... | collective-permute-start | bytes 776 | tf_op jit(solution)/shard_map/ppermute | solution.py:550
  12.9 2.0 %shard_map.149.factor_ref = f32[8,56,128]{2,1,0:T(8,128)} custom-call(f32[8,2,40,80]{3,2,1,0:T(8,128)} %bitcast.8), custom_call_target="tpu_custom_call" | custom-call | tf_op jit(solution)/shard_map/pallas_call | solution.py:391
  14.9 0.6 maximum_select_fusion.temporal_ref
  15.5 1.9 %shard_map.150.after_ref = bf16[8,2,56,128]{3,2,1,0:T(8,128)(2,1)} custom-call(f32[8,2,8]{2,1,0:T(2,128)} %maximum_select_fusion.temporal_ref, f32[8,56,128]{2,1,0:T(8,128)} %shard_map.149.factor_ref), custom_call_target="tpu_custom_call" | custom-call | tf_op jit(solution)/shard_map/pallas_call | solution.py:435
  17.4 13.8 %all_to_all.15.refs_0_ = bf16[8,2,56,128]{3,2,1,0:T(8,128)(2,1)} all-to-all(bf16[8,2,56,128]{3,2,1,0:T(8,128)(2,1)} %shard_map.150.after_ref), channel_id=1, replica_groups=mesh['frame'=8,'coil'=4] {'frame'}, dimensions={0} | all-to-all | bytes 458752 | tf_op jit(solution)/shard_map/all_to_all | solution.py:597
  31.3 1.5 %collective-permute-start.4 = (bf16[8,2,56,128]{3,2,1,0:T(8,128)(2,1)}, bf16[8,2,56,128]{3,2,1,0:T(8,128)(2,1)}, u32[]{:S(2)}, u32[]{:S(2)}) collective-permute-start(bf16[8,2,56,128]{3,2,1,0:T(8,128)(2,1)} %all_to_all.15.refs_0_), channel_id=1, source_target_pairs={{0,2},{1,3},{2,0},{3,1},{4,6},{5,7},{6,4},{7,5},{8,10},{9,11},{10,... | collective-permute-start | bytes 688136 | tf_op jit(solution)/shard_map/ppermute | solution.py:550
  32.8 4.8 %collective-permute-done.4.refs_2_ = bf16[8,2,56,128]{3,2,1,0:T(8,128)(2,1)} collective-permute-done((bf16[8,2,56,128]{3,2,1,0:T(8,128)(2,1)}, bf16[8,2,56,128]{3,2,1,0:T(8,128)(2,1)}, u32[]{:S(2)}, u32[]{:S(2)}) %collective-permute-start.4) | collective-permute-done | bytes 229408 | tf_op jit(solution)/shard_map/ppermute | solution.py:550
  37.6 7.1 %shard_map.151 = (f32[2,320,640]{2,1,0:T(8,128)}, f32[2,320,640]{2,1,0:T(8,128)}, f32[2,8,640]{2,1,0:T(8,128)}, bf16[2,2,320,384]{3,2,1,0:T(8,128)(2,1)}) custom-call(s32[2,640,640]{2,1,0:T(8,128)} %index_ref.1, f32[2,8]{1,0:T(2,128)} %level_ref.1, bf16[2,2,320,320]{3,2,1,0:T(8,128)(2,1)} %sens_ref.1, bf16[320,320]{1,0:T(8,128)(2,1)} %constant.81.clone.row_ref, ...), custom_call_target="tpu_custom_call" | custom-call | flops 1572864000 | bytes 16777216 | tf_op jit(solution)/shard_map/pallas_call | solution.py:503
  44.7 16.0 %shard_map.152 = (f32[8,56,128]{2,1,0:T(8,128)}, f32[8,56,128]{2,1,0:T(8,128)}, f32[8,56,128]{2,1,0:T(8,128)}, f32[8,56,128]{2,1,0:T(8,128)}) custom-call(s32[1]{0:T(128)} %bitcast.2.me_ref, bf16[8,2,56,128]{3,2,1,0:T(8,128)(2,1)} %all_to_all.15.refs_0_, bf16[8,2,56,128]{3,2,1,0:T(8,128)(2,1)} %collective-permute-done.3.refs_1_, ...), custom_call_target="tpu_custom_call" | custom-call | flops 6291456000 | bytes 8388608 | tf_op jit(solution)/shard_map/pallas_call | solution.py:318
  60.7 16.3 %shard_map.153 = (f32[8,56,128]{2,1,0:T(8,128)}, f32[8,56,128]{2,1,0:T(8,128)}, f32[8,56,128]{2,1,0:T(8,128)}, f32[8,56,128]{2,1,0:T(8,128)}) custom-call(s32[1]{0:T(128)} %bitcast.2.me_ref, bf16[8,2,56,128]{3,2,1,0:T(8,128)(2,1)} %all_to_all.15.refs_0_, bf16[8,2,56,128]{3,2,1,0:T(8,128)(2,1)} %collective-permute-done.3.refs_1_, ...), custom_call_target="tpu_custom_call" | custom-call | flops 6291456000 | bytes 8388608 | tf_op jit(solution)/shard_map/pallas_call | solution.py:318
  77.0 0.6 collective-permute-start.10
  77.6 1.5 %collective-permute-start.7 = (f32[8,56,128]{2,1,0:T(8,128)S(1)}, f32[8,56,128]{2,1,0:T(8,128)S(1)}, u32[]{:S(2)}, u32[]{:S(2)}) collective-permute-start(f32[8,56,128]{2,1,0:T(8,128)S(1)} %copy-done.3), channel_id=1, source_target_pairs={{0,2},{1,3},{2,0},{3,1},{4,6},{5,7},{6,4},{7,5},{8,10},{9,11},{10,... | collective-permute-start | bytes 688136 | tf_op jit(solution)/shard_map/ppermute | solution.py:550
  79.1 0.3 collective-permute-start.8
  79.4 0.4 collective-permute-start.9
  79.8 1.0 add.38
  80.7 1.6 %collective-permute-start.11 = (f32[8,56,128]{2,1,0:T(8,128)S(1)}, f32[8,56,128]{2,1,0:T(8,128)S(1)}, u32[]{:S(2)}, u32[]{:S(2)}) collective-permute-start(f32[8,56,128]{2,1,0:T(8,128)S(1)} %add.38), channel_id=1, source_target_pairs={{0,2},{1,3},{2,0},{3,1},{4,6},{5,7},{6,4},{7,5},{8,10},{9,11},{10,... | collective-permute-start | bytes 688136 | tf_op jit(solution)/shard_map/ppermute | solution.py:550
  82.3 3.8 %collective-permute-done.7 = f32[8,56,128]{2,1,0:T(8,128)S(1)} collective-permute-done((f32[8,56,128]{2,1,0:T(8,128)S(1)}, f32[8,56,128]{2,1,0:T(8,128)S(1)}, u32[]{:S(2)}, u32[]{:S(2)}) %collective-permute-start.7) | collective-permute-done | bytes 229408 | tf_op jit(solution)/shard_map/ppermute | solution.py:550
  86.1 3.9 %collective-permute-done.8 = f32[8,56,128]{2,1,0:T(8,128)S(1)} collective-permute-done((f32[8,56,128]{2,1,0:T(8,128)S(1)}, f32[8,56,128]{2,1,0:T(8,128)S(1)}, u32[]{:S(2)}, u32[]{:S(2)}) %collective-permute-start.8) | collective-permute-done | bytes 229408 | tf_op jit(solution)/shard_map/ppermute | solution.py:550
  90.1 5.3 %collective-permute-done.11 = f32[8,56,128]{2,1,0:T(8,128)S(1)} collective-permute-done((f32[8,56,128]{2,1,0:T(8,128)S(1)}, f32[8,56,128]{2,1,0:T(8,128)S(1)}, u32[]{:S(2)}, u32[]{:S(2)}) %collective-permute-start.11) | collective-permute-done | bytes 229408 | tf_op jit(solution)/shard_map/ppermute | solution.py:550
  95.5 16.3 %all_to_all.16.residual_ref = f32[8,2,56,128]{3,2,1,0:T(8,128)} all-to-all(f32[8,2,56,128]{3,2,1,0:T(8,128)S(1)} %pad_maximum_fusion), channel_id=1, replica_groups=mesh['frame'=8,'coil'=4] {'frame'}, dimensions={0} | all-to-all | bytes 917504 | tf_op jit(solution)/shard_map/all_to_all | solution.py:597
  111.8 2.4 %shard_map.154 = (f32[8,56,128]{2,1,0:T(8,128)}, bf16[8,2,56,128]{3,2,1,0:T(8,128)(2,1)}) custom-call(f32[8,2,8]{2,1,0:T(2,128)} %maximum_select_fusion.temporal_ref, f32[8,56,128]{2,1,0:T(8,128)} %shard_map.149.factor_ref, f32[8,2,56,128]{3,2,1,0:T(8,128)} %all_to_all.16.residual_ref), custom_call_target="tpu_custom_call" | custom-call | tf_op jit(solution)/shard_map/pallas_call | solution.py:445
  114.1 11.7 %all_to_all.17.refs_0_ = bf16[8,2,56,128]{3,2,1,0:T(8,128)(2,1)S(1)} all-to-all(bf16[8,2,56,128]{3,2,1,0:T(8,128)(2,1)} %get-tuple-element.29), channel_id=1, replica_groups=mesh['frame'=8,'coil'=4] {'frame'}, dimensions={0} | all-to-all | bytes 458752 | tf_op jit(solution)/shard_map/all_to_all | solution.py:597
  125.8 1.5 %collective-permute-start.12 = (bf16[8,2,56,128]{3,2,1,0:T(8,128)(2,1)S(1)}, bf16[8,2,56,128]{3,2,1,0:T(8,128)(2,1)S(1)}, u32[]{:S(2)}, u32[]{:S(2)}) collective-permute-start(bf16[8,2,56,128]{3,2,1,0:T(8,128)(2,1)S(1)} %all_to_all.17.refs_0_), channel_id=1, source_target_pairs={{0,2},{1,3},{2,0},{3,1},{4,6},{5,7},{6,4},{7,5},{8,10},{9,11},{10,... | collective-permute-start | bytes 688136 | tf_op jit(solution)/shard_map/ppermute | solution.py:550
  127.3 4.5 %collective-permute-done.12.refs_0_ = bf16[8,2,56,128]{3,2,1,0:T(8,128)(2,1)S(1)} collective-permute-done((bf16[8,2,56,128]{3,2,1,0:T(8,128)(2,1)S(1)}, bf16[8,2,56,128]{3,2,1,0:T(8,128)(2,1)S(1)}, u32[]{:S(2)}, u32[]{:S(2)}) %collective-permute-start.12) | collective-permute-done | bytes 229408 | tf_op jit(solution)/shard_map/ppermute | solution.py:550
  131.9 2.0 %shard_map.155 = f32[8,2,40,80]{3,2,1,0:T(8,128)} custom-call(f32[8,56,128]{2,1,0:T(8,128)} %get-tuple-element.28.packed_ref), custom_call_target="tpu_custom_call" | custom-call | tf_op jit(solution)/shard_map/pallas_call | solution.py:403
  133.9 1.1 shard_map.156.refs_2_
  135.0 1.1 shard_map.157
  (27 shorter events, 0.3 us)
Async XLA Ops:
  0.6 4.8 %collective-permute-start = (f32[1,2,8]{2,1,0:T(2,128)}, f32[1,2,8]{2,1,0:T(2,128)S(1)}, u32[]{:S(2)}, u32[]{:S(2)}) collective-permute-start(f32[1,2,8]{2,1,0:T(2,128)} %bitcast.10), channel_id=1, source_target_pairs={{0,4},{4,0},{8,12},{12,8},{16,20},{20,16},{24,28},{28,24},{1,5},{5... | collective-permute-start | bytes 200 | tf_op jit(solution)/shard_map/ppermute | solution.py:550
  6.2 3.6 %collective-permute-start.1 = (f32[2,2,8]{2,1,0:T(2,128)S(1)}, f32[2,2,8]{2,1,0:T(2,128)S(1)}, u32[]{:S(2)}, u32[]{:S(2)}) collective-permute-start(f32[2,2,8]{2,1,0:T(2,128)S(1)} %maximum_select_fusion.2), channel_id=1, source_target_pairs={{0,8},{4,12},{8,0},{12,4},{16,24},{20,28},{24,16},{28,20},{1,9},{5... | collective-permute-start | bytes 392 | tf_op jit(solution)/shard_map/ppermute | solution.py:550
  9.9 5.1 %collective-permute-start.2 = (f32[4,2,8]{2,1,0:T(2,128)S(1)}, f32[4,2,8]{2,1,0:T(2,128)S(1)}, u32[]{:S(2)}, u32[]{:S(2)}) collective-permute-start(f32[4,2,8]{2,1,0:T(2,128)S(1)} %maximum_select_fusion.1), channel_id=1, source_target_pairs={{0,16},{4,20},{8,24},{12,28},{16,0},{20,4},{24,8},{28,12},{1,17},{... | collective-permute-start | bytes 776 | tf_op jit(solution)/shard_map/ppermute | solution.py:550
  31.3 6.3 %collective-permute-start.4 = (bf16[8,2,56,128]{3,2,1,0:T(8,128)(2,1)}, bf16[8,2,56,128]{3,2,1,0:T(8,128)(2,1)}, u32[]{:S(2)}, u32[]{:S(2)}) collective-permute-start(bf16[8,2,56,128]{3,2,1,0:T(8,128)(2,1)} %all_to_all.15.refs_0_), channel_id=1, source_target_pairs={{0,2},{1,3},{2,0},{3,1},{4,6},{5,7},{6,4},{7,5},{8,10},{9,11},{10,... | collective-permute-start | bytes 688136 | tf_op jit(solution)/shard_map/ppermute | solution.py:550
  32.8 11.9 %collective-permute-start.3 = (bf16[8,2,56,128]{3,2,1,0:T(8,128)(2,1)}, bf16[8,2,56,128]{3,2,1,0:T(8,128)(2,1)}, u32[]{:S(2)}, u32[]{:S(2)}) collective-permute-start(bf16[8,2,56,128]{3,2,1,0:T(8,128)(2,1)} %all_to_all.15.refs_0_), channel_id=1, source_target_pairs={{0,1},{1,0},{2,3},{3,2},{4,5},{5,4},{6,7},{7,6},{8,9},{9,8},{10,11... | collective-permute-start | bytes 688136 | tf_op jit(solution)/shard_map/ppermute | solution.py:550
  37.6 7.1 %collective-permute-start.5 = (bf16[8,2,56,128]{3,2,1,0:T(8,128)(2,1)}, bf16[8,2,56,128]{3,2,1,0:T(8,128)(2,1)}, u32[]{:S(2)}, u32[]{:S(2)}) collective-permute-start(bf16[8,2,56,128]{3,2,1,0:T(8,128)(2,1)} %collective-permute-done.4.refs_2_), channel_id=1, source_target_pairs={{0,1},{1,0},{2,3},{3,2},{4,5},{5,4},{6,7},{7,6},{8,9},{9,8},{10,11... | collective-permute-start | bytes 688136 | tf_op jit(solution)/shard_map/ppermute | solution.py:550
  60.7 16.9 %copy-start.4 = (f32[8,56,128]{2,1,0:T(8,128)S(1)}, f32[8,56,128]{2,1,0:T(8,128)}, u32[]{:S(2)}) copy-start(f32[8,56,128]{2,1,0:T(8,128)} %get-tuple-element.21) | copy-start | bytes 688132
  60.7 17.0 %copy-start.3 = (f32[8,56,128]{2,1,0:T(8,128)S(1)}, f32[8,56,128]{2,1,0:T(8,128)}, u32[]{:S(2)}) copy-start(f32[8,56,128]{2,1,0:T(8,128)} %get-tuple-element.22) | copy-start | bytes 688132
  60.7 18.4 %copy-start.2 = (f32[8,56,128]{2,1,0:T(8,128)S(1)}, f32[8,56,128]{2,1,0:T(8,128)}, u32[]{:S(2)}) copy-start(f32[8,56,128]{2,1,0:T(8,128)} %get-tuple-element.23) | copy-start | bytes 688132
  60.7 29.3 %copy-start.1 = (f32[8,56,128]{2,1,0:T(8,128)S(1)}, f32[8,56,128]{2,1,0:T(8,128)}, u32[]{:S(2)}) copy-start(f32[8,56,128]{2,1,0:T(8,128)} %get-tuple-element.20.refs_14_) | copy-start | bytes 688132
  77.0 18.4 %copy-start = (f32[8,56,128]{2,1,0:T(8,128)S(1)}, f32[8,56,128]{2,1,0:T(8,128)}, u32[]{:S(2)}) copy-start(f32[8,56,128]{2,1,0:T(8,128)} %get-tuple-element.24) | copy-start | bytes 688132
  77.0 2.8 %collective-permute-start.10 = (f32[8,56,128]{2,1,0:T(8,128)}, f32[8,56,128]{2,1,0:T(8,128)S(1)}, u32[]{:S(2)}, u32[]{:S(2)}) collective-permute-start(f32[8,56,128]{2,1,0:T(8,128)} %get-tuple-element.27), channel_id=1, source_target_pairs={{0,1},{1,0},{2,3},{3,2},{4,5},{5,4},{6,7},{7,6},{8,9},{9,8},{10,11... | collective-permute-start | bytes 688136 | tf_op jit(solution)/shard_map/ppermute | solution.py:550
  77.5 4.8 %collective-permute-start.6 = (f32[8,56,128]{2,1,0:T(8,128)S(1)}, f32[8,56,128]{2,1,0:T(8,128)S(1)}, u32[]{:S(2)}, u32[]{:S(2)}) collective-permute-start(f32[8,56,128]{2,1,0:T(8,128)S(1)} %copy-done.4), channel_id=1, source_target_pairs={{0,1},{1,0},{2,3},{3,2},{4,5},{5,4},{6,7},{7,6},{8,9},{9,8},{10,11... | collective-permute-start | bytes 688136 | tf_op jit(solution)/shard_map/ppermute | solution.py:550
  77.6 8.5 %collective-permute-start.7 = (f32[8,56,128]{2,1,0:T(8,128)S(1)}, f32[8,56,128]{2,1,0:T(8,128)S(1)}, u32[]{:S(2)}, u32[]{:S(2)}) collective-permute-start(f32[8,56,128]{2,1,0:T(8,128)S(1)} %copy-done.3), channel_id=1, source_target_pairs={{0,2},{1,3},{2,0},{3,1},{4,6},{5,7},{6,4},{7,5},{8,10},{9,11},{10,... | collective-permute-start | bytes 688136 | tf_op jit(solution)/shard_map/ppermute | solution.py:550
  79.1 10.9 %collective-permute-start.8 = (f32[8,56,128]{2,1,0:T(8,128)S(1)}, f32[8,56,128]{2,1,0:T(8,128)S(1)}, u32[]{:S(2)}, u32[]{:S(2)}) collective-permute-start(f32[8,56,128]{2,1,0:T(8,128)S(1)} %copy-done.2), channel_id=1, source_target_pairs={{0,3},{1,2},{2,1},{3,0},{4,7},{5,6},{6,5},{7,4},{8,11},{9,10},{10,... | collective-permute-start | bytes 688136 | tf_op jit(solution)/shard_map/ppermute | solution.py:550
  79.4 10.7 %collective-permute-start.9 = (f32[8,56,128]{2,1,0:T(8,128)}, f32[8,56,128]{2,1,0:T(8,128)S(1)}, u32[]{:S(2)}, u32[]{:S(2)}) collective-permute-start(f32[8,56,128]{2,1,0:T(8,128)} %get-tuple-element.25), channel_id=1, source_target_pairs={{0,1},{1,0},{2,3},{3,2},{4,5},{5,4},{6,7},{7,6},{8,9},{9,8},{10,11... | collective-permute-start | bytes 688136 | tf_op jit(solution)/shard_map/ppermute | solution.py:550
  80.7 14.6 %collective-permute-start.11 = (f32[8,56,128]{2,1,0:T(8,128)S(1)}, f32[8,56,128]{2,1,0:T(8,128)S(1)}, u32[]{:S(2)}, u32[]{:S(2)}) collective-permute-start(f32[8,56,128]{2,1,0:T(8,128)S(1)} %add.38), channel_id=1, source_target_pairs={{0,2},{1,3},{2,0},{3,1},{4,6},{5,7},{6,4},{7,5},{8,10},{9,11},{10,... | collective-permute-start | bytes 688136 | tf_op jit(solution)/shard_map/ppermute | solution.py:550
  125.8 6.0 %collective-permute-start.12 = (bf16[8,2,56,128]{3,2,1,0:T(8,128)(2,1)S(1)}, bf16[8,2,56,128]{3,2,1,0:T(8,128)(2,1)S(1)}, u32[]{:S(2)}, u32[]{:S(2)}) collective-permute-start(bf16[8,2,56,128]{3,2,1,0:T(8,128)(2,1)S(1)} %all_to_all.17.refs_0_), channel_id=1, source_target_pairs={{0,2},{1,3},{2,0},{3,1},{4,6},{5,7},{6,4},{7,5},{8,10},{9,11},{10,... | collective-permute-start | bytes 688136 | tf_op jit(solution)/shard_map/ppermute | solution.py:550
  127.3 6.6 %collective-permute-start.14 = (bf16[8,2,56,128]{3,2,1,0:T(8,128)(2,1)S(1)}, bf16[8,2,56,128]{3,2,1,0:T(8,128)(2,1)S(1)}, u32[]{:S(2)}, u32[]{:S(2)}) collective-permute-start(bf16[8,2,56,128]{3,2,1,0:T(8,128)(2,1)S(1)} %all_to_all.17.refs_0_), channel_id=1, source_target_pairs={{0,1},{1,0},{2,3},{3,2},{4,5},{5,4},{6,7},{7,6},{8,9},{9,8},{10,11... | collective-permute-start | bytes 688136 | tf_op jit(solution)/shard_map/ppermute | solution.py:550
  131.9 3.1 %collective-permute-start.13 = (bf16[8,2,56,128]{3,2,1,0:T(8,128)(2,1)S(1)}, bf16[8,2,56,128]{3,2,1,0:T(8,128)(2,1)S(1)}, u32[]{:S(2)}, u32[]{:S(2)}) collective-permute-start(bf16[8,2,56,128]{3,2,1,0:T(8,128)(2,1)S(1)} %collective-permute-done.12.refs_0_), channel_id=1, source_target_pairs={{0,1},{1,0},{2,3},{3,2},{4,5},{5,4},{6,7},{7,6},{8,9},{9,8},{10,11... | collective-permute-start | bytes 688136 | tf_op jit(solution)/shard_map/ppermute | solution.py:550
